TPU v7x, 32 devices: a whole 2x2x4 slice. The times are simulated.
32 devices in a mesh: ctx: 16 (over z, y, core), fsdp: 2 (over x).
Axes of the slice: x: 2, y: 2, z: 4, core: 2. Of those that a mesh axis runs over, the one named last changes fastest.
Arguments:
- tokens: bfloat16 [2, 2048, 1024], P('fsdp', 'ctx'), may hold values from -6 to 6
- w_qkv: bfloat16 [1024, 3072], P('fsdp'), may hold values from -0.1875 to 0.1875
- w_out: bfloat16 [1024, 1024], P('fsdp'), may hold values from -0.375 to 0.375
- w_up: bfloat16 [1024, 4096], P('fsdp'), may hold values from -0.1875 to 0.1875
- w_down: bfloat16 [4096, 1024], P('fsdp'), may hold values from -0.09375 to 0.09375
- w_time: bfloat16 [256, 2048], P('fsdp'), may hold values from -0.375 to 0.375
- gain_one: bfloat16 [1024], P('fsdp'), may hold values from 0.5 to 1.5
- bias_one: bfloat16 [1024], P('fsdp'), may hold values from -3 to 3
- gain_two: bfloat16 [1024], P('fsdp'), may hold values from 0.5 to 1.5
- bias_two: bfloat16 [1024], P('fsdp'), may hold values from -3 to 3
- bias_up: bfloat16 [4096], P('fsdp'), may hold values from -3 to 3
- bias_down: bfloat16 [1024], P('fsdp'), may hold values from -3 to 3
- lengths: int32 [2, 1], P('fsdp'), may hold values from 1024 to 2048, as said below
- time_steps: int32 [2, 1], P('fsdp'), may hold values from 0 to 999
- cotangent: bfloat16 [2, 2048, 1024], P('fsdp', 'ctx'), may hold values from -6 to 6
Outputs:
- output: bfloat16 [2, 2048, 1024], P('fsdp', 'ctx')
- grad_tokens: bfloat16 [2, 2048, 1024], P('fsdp', 'ctx')
- grad_qkv: float32 [1024, 3072], P('fsdp')
- grad_out: float32 [1024, 1024], P('fsdp')
- grad_up: float32 [1024, 4096], P('fsdp')
- grad_down: float32 [4096, 1024], P('fsdp')
- grad_time: float32 [256, 2048], P('fsdp')
- grad_gain_one: float32 [1024], P('fsdp')
- grad_bias_one: float32 [1024], P('fsdp')
- grad_gain_two: float32 [1024], P('fsdp')
- grad_bias_two: float32 [1024], P('fsdp')
- grad_bias_up: float32 [4096], P('fsdp')
- grad_bias_down: float32 [1024], P('fsdp')
Inputs may be any that keep to these rules, and one draw needn't show every extreme that they name: The 1 lengths of a group add up to at most 2048; the group's tokens after them are padding; in every group some sequence has the largest length.
All inputs are finite; a program needn't handle non-finite values.
Results may differ from a plain program's by a relative error of at most 0.025.
Values may be sent and summed in bfloat16 or wider, within the bound.
No kernel may reach another device: no remote copies, remote signals or barrier semaphores. Data moves between devices by JAX's collectives and lax.ppermute only.
A program may use at most 256 MiB of HBM per device.

v0:
```python
import math

import jax
import jax.numpy as jnp
from jax import lax
from jax.sharding import PartitionSpec as P

HEADS = 16


HIGH = lax.Precision.HIGHEST
EPSILON = 1e-05
NEGATIVE = -1e30


def layout(seq_lengths, offsets):
    ends = jnp.cumsum(seq_lengths)
    starts = jnp.concatenate([jnp.zeros((1,), jnp.int32), ends])
    segment = jnp.sum((offsets[:, None] >= ends[None, :]).astype(jnp.int32), axis=1)
    onehot = segment[:, None] == jnp.arange(seq_lengths.shape[0] + 1, dtype=jnp.int32)[None, :]
    begin = jnp.sum(jnp.where(onehot, starts[None, :], 0), axis=1)
    return (segment, onehot, offsets - begin)


def embed(steps_given, embed_width):
    half_width = embed_width // 2
    freq = jnp.exp(-math.log(10000.0) * jnp.arange(half_width, dtype=jnp.float32) / half_width)
    angle = steps_given.astype(jnp.float32)[..., None] * freq
    return jnp.concatenate([jnp.sin(angle), jnp.cos(angle)], axis=-1)


def rotary(values, position, heads):
    width = values.shape[-1]
    half_width = width // heads // 2
    inverse = jnp.exp(-math.log(10000.0) * jnp.arange(half_width, dtype=jnp.float32) / half_width)
    angle = position.astype(jnp.float32)[..., None] * inverse
    cosine = jnp.cos(angle)[..., None, :]
    sine = jnp.sin(angle)[..., None, :]
    split = values.reshape(values.shape[:-1] + (heads, 2, half_width))
    upper = split[..., 0, :]
    lower = split[..., 1, :]
    turned = jnp.stack([upper * cosine - lower * sine, lower * cosine + upper * sine], axis=-2)
    return turned.reshape(values.shape)


def normalize(values):
    centre = jnp.mean(values, axis=-1, keepdims=True)
    centered = values - centre
    spread = jnp.mean(centered * centered, axis=-1, keepdims=True)
    return centered * lax.rsqrt(spread + EPSILON)


def modulate(values, gain, bias, film_tok):
    width = values.shape[-1]
    return normalize(values) * (gain + film_tok[:, :width]) + (bias + film_tok[:, width:])


def affine(values, gain, bias):
    return normalize(values) * gain + bias


def gelu_exact(values):
    return jax.nn.gelu(values, approximate=False)


def split_heads(values, heads):
    return values.reshape(values.shape[0], heads, values.shape[1] // heads)


def contract_rows(left, right):
    return lax.dot_general(
        left, right, (((0,), (0,)), ((), ())), preferred_element_type=jnp.float32
    )


def contract_cols(left, right):
    return lax.dot_general(
        left, right, (((1,), (1,)), ((), ())), preferred_element_type=jnp.float32
    )


def body(
    tokens,
    w_qkv,
    w_out,
    w_up,
    w_down,
    w_time,
    gain_one,
    bias_one,
    gain_two,
    bias_two,
    bias_up,
    bias_down,
    lengths,
    time_steps,
    cotangent,
):
    gathered = (
        lax.all_gather(w_qkv, "fsdp", axis=0, tiled=True),
        lax.all_gather(w_out, "fsdp", axis=0, tiled=True),
        lax.all_gather(w_up, "fsdp", axis=0, tiled=True),
        lax.all_gather(w_down, "fsdp", axis=0, tiled=True),
        lax.all_gather(w_time, "fsdp", axis=0, tiled=True),
        lax.all_gather(gain_one, "fsdp", axis=0, tiled=True),
        lax.all_gather(bias_one, "fsdp", axis=0, tiled=True),
        lax.all_gather(gain_two, "fsdp", axis=0, tiled=True),
        lax.all_gather(bias_two, "fsdp", axis=0, tiled=True),
        lax.all_gather(bias_up, "fsdp", axis=0, tiled=True),
        lax.all_gather(bias_down, "fsdp", axis=0, tiled=True),
    )
    full_qkv, full_out, full_up, full_down, full_time = (
        gathered[0],
        gathered[1],
        gathered[2],
        gathered[3],
        gathered[4],
    )
    gain_first = gathered[5].astype(jnp.float32)
    bias_first = gathered[6].astype(jnp.float32)
    gain_second = gathered[7].astype(jnp.float32)
    bias_second = gathered[8].astype(jnp.float32)
    bias_hidden = gathered[9].astype(jnp.float32)
    bias_output = gathered[10].astype(jnp.float32)
    row_count = tokens.shape[1]
    width = tokens.shape[2]
    heads = HEADS
    head_size = width // heads
    scale = float(head_size) ** (-0.5)
    seq_lengths = lengths[0]
    seq_count = seq_lengths.shape[0]
    offsets = lax.axis_index("ctx") * row_count + jnp.arange(row_count, dtype=jnp.int32)
    segment, onehot, position = layout(seq_lengths, offsets)
    live = (segment < seq_count).astype(jnp.float32)
    onehot_float = onehot.astype(jnp.float32)
    inputs = tokens[0].astype(jnp.float32)
    temb = embed(time_steps[0], full_time.shape[0]).astype(jnp.bfloat16)
    film = jnp.dot(temb, full_time, preferred_element_type=jnp.float32)
    film_ext = jnp.concatenate([film, jnp.zeros((1, film.shape[1]), jnp.float32)], axis=0)
    film_tok = jnp.dot(onehot_float, film_ext, precision=HIGH)
    norm_one, pull_one = jax.vjp(modulate, inputs, gain_first, bias_first, film_tok)
    norm_one_b = norm_one.astype(jnp.bfloat16)
    mixed = jnp.dot(norm_one_b, full_qkv, preferred_element_type=jnp.float32)

    def turn_pair(query_raw, key_raw):
        return (rotary(query_raw, position, heads), rotary(key_raw, position, heads))

    turned, pull_turn = jax.vjp(turn_pair, mixed[:, :width], mixed[:, width : 2 * width])
    query = turned[0].astype(jnp.bfloat16)
    key = turned[1].astype(jnp.bfloat16)
    value = mixed[:, 2 * width :].astype(jnp.bfloat16)
    query_heads = split_heads(query, heads)
    key_heads = split_heads(key, heads)
    value_heads = split_heads(value, heads)
    row_max = jnp.full((heads, row_count), NEGATIVE, jnp.float32)
    weighted = jnp.zeros((row_count, heads, head_size), jnp.float32)
    piece_keys = lax.all_gather(key, "ctx", axis=0, tiled=True)
    piece_values = lax.all_gather(value, "ctx", axis=0, tiled=True)
    piece_rows = piece_keys.shape[0]
    piece_segment = layout(seq_lengths, jnp.arange(piece_rows, dtype=jnp.int32))[0]
    scaled = (
        jnp.einsum(
            "qhd,khd->hqk",
            query_heads,
            split_heads(piece_keys, heads),
            preferred_element_type=jnp.float32,
        )
        * scale
    )
    matches = (segment[:, None] == piece_segment[None, :])[None]
    masked = jnp.where(matches, scaled, NEGATIVE)
    new_max = jnp.maximum(row_max, jnp.max(masked, axis=2))
    weights_now = jnp.where(matches, jnp.exp(masked - new_max[:, :, None]), 0.0)
    decay = jnp.exp(row_max - new_max)
    row_sum = jnp.sum(weights_now, axis=2)
    partial_value = jnp.einsum(
        "hqk,khd->qhd",
        weights_now.astype(jnp.bfloat16),
        split_heads(piece_values, heads),
        preferred_element_type=jnp.float32,
    )
    weighted = weighted * decay.T[:, :, None] + partial_value
    row_max, row_sum, weighted = (new_max, row_sum, weighted)
    attended_heads = weighted / row_sum.T[:, :, None]
    log_total = row_max + jnp.log(row_sum)
    attended_b = attended_heads.reshape(row_count, width).astype(jnp.bfloat16)
    resid = inputs + jnp.dot(attended_b, full_out, preferred_element_type=jnp.float32)
    norm_two, pull_two = jax.vjp(affine, resid, gain_second, bias_second)
    norm_two_b = norm_two.astype(jnp.bfloat16)
    pre = jnp.dot(norm_two_b, full_up, preferred_element_type=jnp.float32) + bias_hidden
    act, pull_act = jax.vjp(gelu_exact, pre)
    act_b = act.astype(jnp.bfloat16)
    branch = jnp.dot(act_b, full_down, preferred_element_type=jnp.float32) + bias_output
    output = (live[:, None] * (resid + branch)).astype(jnp.bfloat16)
    again = (
        lax.all_gather(w_qkv, "fsdp", axis=0, tiled=True),
        lax.all_gather(w_out, "fsdp", axis=0, tiled=True),
        lax.all_gather(w_up, "fsdp", axis=0, tiled=True),
        lax.all_gather(w_down, "fsdp", axis=0, tiled=True),
        lax.all_gather(w_time, "fsdp", axis=0, tiled=True),
        lax.all_gather(gain_one, "fsdp", axis=0, tiled=True),
        lax.all_gather(bias_one, "fsdp", axis=0, tiled=True),
        lax.all_gather(gain_two, "fsdp", axis=0, tiled=True),
        lax.all_gather(bias_two, "fsdp", axis=0, tiled=True),
        lax.all_gather(bias_up, "fsdp", axis=0, tiled=True),
        lax.all_gather(bias_down, "fsdp", axis=0, tiled=True),
    )
    back_qkv, back_out, back_up, back_down = (again[0], again[1], again[2], again[3])
    grad_y = cotangent[0].astype(jnp.float32) * live[:, None]
    grad_bias_down = jnp.sum(grad_y, axis=0)
    grad_y_b = grad_y.astype(jnp.bfloat16)
    grad_down = contract_rows(act_b, grad_y_b)
    grad_act = contract_cols(grad_y_b, back_down)
    grad_pre = pull_act(grad_act)[0]
    grad_bias_up = jnp.sum(grad_pre, axis=0)
    grad_pre_b = grad_pre.astype(jnp.bfloat16)
    grad_up = contract_rows(norm_two_b, grad_pre_b)
    grad_norm_two = contract_cols(grad_pre_b, back_up)
    grad_resid_norm, grad_gain_two, grad_bias_two = pull_two(grad_norm_two)
    grad_resid = grad_y + grad_resid_norm
    grad_resid_b = grad_resid.astype(jnp.bfloat16)
    grad_out = contract_rows(attended_b, grad_resid_b)
    grad_att = contract_cols(grad_resid_b, back_out).astype(jnp.bfloat16)
    grad_att_heads = split_heads(grad_att, heads)
    delta = jnp.einsum(
        "qhd,qhd->hq", grad_att_heads.astype(jnp.float32), attended_heads, precision=HIGH
    )
    piece_keys = lax.all_gather(key, "ctx", axis=0, tiled=True)
    piece_values = lax.all_gather(value, "ctx", axis=0, tiled=True)
    piece_rows = piece_keys.shape[0]
    piece_segment = layout(seq_lengths, jnp.arange(piece_rows, dtype=jnp.int32))[0]
    keys_split = split_heads(piece_keys, heads)
    scaled = (
        jnp.einsum("qhd,khd->hqk", query_heads, keys_split, preferred_element_type=jnp.float32)
        * scale
    )
    matches = (segment[:, None] == piece_segment[None, :])[None]
    prob = jnp.where(matches, jnp.exp(scaled - log_total[:, :, None]), 0.0)
    grad_prob = jnp.einsum(
        "qhd,khd->hqk",
        grad_att_heads,
        split_heads(piece_values, heads),
        preferred_element_type=jnp.float32,
    )
    grad_score = (prob * (grad_prob - delta[:, :, None])).astype(jnp.bfloat16)
    grad_query = (
        jnp.einsum("hqk,khd->qhd", grad_score, keys_split, preferred_element_type=jnp.float32)
        * scale
    )
    stats_max, stats_delta = (
        lax.all_gather(log_total.T, "ctx", axis=0, tiled=True),
        lax.all_gather(delta.T, "ctx", axis=0, tiled=True),
    )
    piece_queries = lax.all_gather(query, "ctx", axis=0, tiled=True)
    piece_grads = lax.all_gather(grad_att, "ctx", axis=0, tiled=True)
    piece_rows = piece_queries.shape[0]
    piece_segment = layout(seq_lengths, jnp.arange(piece_rows, dtype=jnp.int32))[0]
    queries_split = split_heads(piece_queries, heads)
    grads_split = split_heads(piece_grads, heads)
    scaled = (
        jnp.einsum("qhd,khd->hqk", queries_split, key_heads, preferred_element_type=jnp.float32)
        * scale
    )
    matches = (piece_segment[:, None] == segment[None, :])[None]
    prob = jnp.where(matches, jnp.exp(scaled - stats_max.T[:, :, None]), 0.0)
    grad_value_now = jnp.einsum(
        "hqk,qhd->khd", prob.astype(jnp.bfloat16), grads_split, preferred_element_type=jnp.float32
    )
    grad_prob = jnp.einsum(
        "qhd,khd->hqk", grads_split, value_heads, preferred_element_type=jnp.float32
    )
    grad_score = (prob * (grad_prob - stats_delta.T[:, :, None])).astype(jnp.bfloat16)
    grad_key_now = (
        jnp.einsum("hqk,qhd->khd", grad_score, queries_split, preferred_element_type=jnp.float32)
        * scale
    )
    grad_turned = pull_turn(
        (grad_query.reshape(row_count, width), grad_key_now.reshape(row_count, width))
    )
    grad_mixed_b = jnp.concatenate(
        [grad_turned[0], grad_turned[1], grad_value_now.reshape(row_count, width)], axis=1
    ).astype(jnp.bfloat16)
    grad_qkv = contract_rows(norm_one_b, grad_mixed_b)
    grad_norm_one = contract_cols(grad_mixed_b, back_qkv)
    grad_inputs_norm, grad_gain_one, grad_bias_one, grad_film_tok = pull_one(grad_norm_one)
    grad_tokens = (grad_resid + grad_inputs_norm).astype(jnp.bfloat16)
    grad_film = lax.dot_general(
        onehot_float, grad_film_tok, (((0,), (0,)), ((), ())), precision=HIGH
    )[:seq_count]
    grad_time = lax.dot_general(
        temb.astype(jnp.float32), grad_film, (((0,), (0,)), ((), ())), precision=HIGH
    )
    shares = (
        lax.psum_scatter(
            grad_qkv.astype(jnp.bfloat16), "fsdp", scatter_dimension=0, tiled=True
        ).astype(jnp.float32),
        lax.psum_scatter(
            grad_out.astype(jnp.bfloat16), "fsdp", scatter_dimension=0, tiled=True
        ).astype(jnp.float32),
        lax.psum_scatter(
            grad_up.astype(jnp.bfloat16), "fsdp", scatter_dimension=0, tiled=True
        ).astype(jnp.float32),
        lax.psum_scatter(
            grad_down.astype(jnp.bfloat16), "fsdp", scatter_dimension=0, tiled=True
        ).astype(jnp.float32),
        lax.psum_scatter(
            grad_time.astype(jnp.bfloat16), "fsdp", scatter_dimension=0, tiled=True
        ).astype(jnp.float32),
        lax.psum_scatter(
            grad_gain_one.astype(jnp.bfloat16), "fsdp", scatter_dimension=0, tiled=True
        ).astype(jnp.float32),
        lax.psum_scatter(
            grad_bias_one.astype(jnp.bfloat16), "fsdp", scatter_dimension=0, tiled=True
        ).astype(jnp.float32),
        lax.psum_scatter(
            grad_gain_two.astype(jnp.bfloat16), "fsdp", scatter_dimension=0, tiled=True
        ).astype(jnp.float32),
        lax.psum_scatter(
            grad_bias_two.astype(jnp.bfloat16), "fsdp", scatter_dimension=0, tiled=True
        ).astype(jnp.float32),
        lax.psum_scatter(
            grad_bias_up.astype(jnp.bfloat16), "fsdp", scatter_dimension=0, tiled=True
        ).astype(jnp.float32),
        lax.psum_scatter(
            grad_bias_down.astype(jnp.bfloat16), "fsdp", scatter_dimension=0, tiled=True
        ).astype(jnp.float32),
    )
    (
        share_qkv,
        share_out,
        share_up,
        share_down,
        share_time,
        share_gone,
        share_bone,
        share_gtwo,
        share_btwo,
        share_bup,
        share_bdown,
    ) = shares
    totals = (
        lax.psum(share_qkv.astype(jnp.bfloat16), "ctx").astype(jnp.float32),
        lax.psum(share_out.astype(jnp.bfloat16), "ctx").astype(jnp.float32),
        lax.psum(share_up.astype(jnp.bfloat16), "ctx").astype(jnp.float32),
        lax.psum(share_down.astype(jnp.bfloat16), "ctx").astype(jnp.float32),
        lax.psum(share_time.astype(jnp.bfloat16), "ctx").astype(jnp.float32),
        lax.psum(share_gone.astype(jnp.bfloat16), "ctx").astype(jnp.float32),
        lax.psum(share_bone.astype(jnp.bfloat16), "ctx").astype(jnp.float32),
        lax.psum(share_gtwo.astype(jnp.bfloat16), "ctx").astype(jnp.float32),
        lax.psum(share_btwo.astype(jnp.bfloat16), "ctx").astype(jnp.float32),
        lax.psum(share_bup.astype(jnp.bfloat16), "ctx").astype(jnp.float32),
        lax.psum(share_bdown.astype(jnp.bfloat16), "ctx").astype(jnp.float32),
    )
    return (
        output[None],
        grad_tokens[None],
        totals[0],
        totals[1],
        totals[2],
        totals[3],
        totals[4],
        totals[5],
        totals[6],
        totals[7],
        totals[8],
        totals[9],
        totals[10],
    )


def solution(mesh):
    in_specs = (
        P("fsdp", "ctx", None),
        P("fsdp", None),
        P("fsdp", None),
        P("fsdp", None),
        P("fsdp", None),
        P("fsdp", None),
        P("fsdp"),
        P("fsdp"),
        P("fsdp"),
        P("fsdp"),
        P("fsdp"),
        P("fsdp"),
        P("fsdp", None),
        P("fsdp", None),
        P("fsdp", "ctx", None),
    )
    out_specs = (
        P("fsdp", "ctx", None),
        P("fsdp", "ctx", None),
        P("fsdp", None),
        P("fsdp", None),
        P("fsdp", None),
        P("fsdp", None),
        P("fsdp", None),
        P("fsdp"),
        P("fsdp"),
        P("fsdp"),
        P("fsdp"),
        P("fsdp"),
        P("fsdp"),
    )
    return jax.shard_map(body, mesh=mesh, in_specs=in_specs, out_specs=out_specs, check_vma=False)
```

profile of v0, /device:TPU:0, one launch (start us, length us, event | category | flops | bytes accessed | tf_op | source)
XLA Modules:
  0.0 1203.4 jit_solution(12869326752963828979)
XLA Ops:
  10.7 5.2 all-gather.1
  15.9 4.3 all-gather
  22.1 11.5 all-gather.15.cloned.1.call-done
  33.6 1.5 fusion.103
  36.0 79.6 %all-gather.17.cloned.1.call-done = bf16[1024,3072]{1,0:T(8,128)(2,1)} async-done(((bf16[512,3072]{1,0:T(8,128)(2,1)}), bf16[1024,3072]{1,0:T(8,128)(2,1)}) %all-gather.17.cloned.1.call-update) | async-done | bytes 6291472 | tf_op jit(solution)/shard_map/all_gather | solution.py:100
  115.6 3.8 fusion.104
  119.4 1.0 fusion.99
  120.5 2.0 copy.53
  122.5 2.0 copy.52
  124.5 2.0 multiply_subtract_fusion
  130.1 4.3 all_gather.67
  135.1 4.3 all-gather.3
  139.4 4.3 all-gather.2
  145.3 35.4 %all-gather.19.cloned.1.call-done = bf16[2048,1024]{0,1:T(8,128)(2,1)} async-done(((bf16[128,1024]{0,1:T(8,128)(2,1)}), bf16[2048,1024]{0,1:T(8,128)(2,1)}) %all-gather.19.cloned.1.call-update) | async-done | bytes 4194320 | tf_op jit(solution)/shard_map/all_gather | solution.py:157
  180.7 4.9 select_reduce_fusion
  185.6 5.0 fusion.1
  190.6 0.8 copy-done
  191.5 40.6 %all-gather.21.cloned.1.call-done = bf16[2048,1024]{1,0:T(8,128)(2,1)} async-done(((bf16[128,1024]{1,0:T(8,128)(2,1)}), bf16[2048,1024]{1,0:T(8,128)(2,1)}) %all-gather.21.cloned.1.call-update) | async-done | bytes 4194320 | tf_op jit(solution)/shard_map/all_gather | solution.py:158
  232.0 6.4 copy.54
  238.5 13.3 %fusion.100 = (bf16[128,16,64]{0,2,1:T(8,128)(2,1)S(1)}, f32[128,16,64]{0,2,1:T(8,128)}) fusion(f32[128,16]{0,1:T(8,128)S(1)} %bitcast.186, bf16[2048,16,64]{0,2,1:T(8,128)(2,1)} %bitcast.155, f32[16,128,2048]{2,1,0:T(8,128)} %copy-done, f32[16,128]{1,0:T(8,128)S(1)} %broadcast_maximum_fusion, pred[128,2048]{1,0:T(8,128)(4,1)S(1)} %broadcast_compare_fusion.1, ...), kind=kOutput, calls=%fused_computation.164 | convolution fusion | flops 558235648 | bytes 22044672 | tf_op jit(solution)/shard_map/hqk,khd->qhd/dot_general | solution.py:176
  251.8 13.3 %all-gather.23.cloned.1.call-done = bf16[1024,1024]{1,0:T(8,128)(2,1)} async-done(((bf16[512,1024]{1,0:T(8,128)(2,1)}), bf16[1024,1024]{1,0:T(8,128)(2,1)}) %all-gather.23.cloned.1.call-update) | async-done | bytes 2097168 | tf_op jit(solution)/shard_map/all_gather | solution.py:101
  265.1 2.1 fusion.101
  267.4 103.1 %all-gather.25.cloned.1.call-done = bf16[1024,4096]{1,0:T(8,128)(2,1)} async-done(((bf16[512,4096]{1,0:T(8,128)(2,1)}), bf16[1024,4096]{1,0:T(8,128)(2,1)}) %all-gather.25.cloned.1.call-update) | async-done | bytes 8388624 | tf_op jit(solution)/shard_map/all_gather | solution.py:102
  370.5 9.1 multiply_convert_fusion.5
  379.6 96.5 %all-gather.27.cloned.1.call-done = bf16[4096,1024]{1,0:T(8,128)(2,1)} async-done(((bf16[2048,1024]{1,0:T(8,128)(2,1)}), bf16[4096,1024]{1,0:T(8,128)(2,1)}) %all-gather.27.cloned.1.call-update) | async-done | bytes 8388624 | tf_op jit(solution)/shard_map/all_gather | solution.py:103
  476.1 10.7 fusion.102
  486.8 3.5 multiply_reduce_fusion
  492.9 1.5 convolution_convert_fusion.4
  495.1 1.0 broadcast_compare_fusion
  496.2 1.8 copy.57
  497.9 1.8 copy.55
  499.7 23.5 %all_gather.71 = f32[2048,16]{0,1:T(8,128)} all-gather(f32[128,16]{0,1:T(8,128)S(1)} %get-tuple-element.63), channel_id=1, replica_groups=mesh['ctx'=16,'fsdp'=2] {'ctx'}, dimensions={0}, use_global_device_ids=true | all-gather | bytes 139264 | tf_op jit(solution)/shard_map/all_gather | solution.py:251
  523.3 1.2 fusion.59
  524.5 19.3 %all_gather.73 = f32[2048,16]{0,1:T(8,128)} all-gather(f32[128,16]{0,1:T(8,128)S(1)} %bitcast.191), channel_id=1, replica_groups=mesh['ctx'=16,'fsdp'=2] {'ctx'}, dimensions={0}, use_global_device_ids=true | all-gather | bytes 139264 | tf_op jit(solution)/shard_map/all_gather | solution.py:252
  543.8 3.0 convolution_convert_fusion.3
  546.8 10.5 fusion.105
  557.4 14.2 %fusion.26 = f32[16,64,128]{2,1,0:T(8,128)} fusion(bf16[2048,16,64]{0,2,1:T(8,128)(2,1)} %bitcast.154, f32[16,128,2048]{2,1,0:T(8,128)} %copy-done, f32[16,128]{1,0:T(8,128)S(1)} %fusion.59, f32[16,128]{1,0:T(8,128)S(1)} %log_add_fusion, pred[128,2048]{1,0:T(8,128)(4,1)S(1)} %broadcast_compare_fusion.1, bf16[128,16,64]{0,2,1:T(8,128)(2,1)} %bitcast.166, ...), kind=kOutput, calls=%fused_computation.43 | convolution fusion | flops 1099038720 | bytes 26230784 | tf_op jit(solution)/shard_map/hqk,khd->qhd/dot_general | solution.py:247
  571.7 12.1 %all-gather.31.cloned.1.call-done = bf16[2048,1024]{1,0:T(8,128)(2,1)} async-done(((bf16[128,1024]{1,0:T(8,128)(2,1)}), bf16[2048,1024]{1,0:T(8,128)(2,1)}) %all-gather.31.cloned.1.call-update) | async-done | bytes 4194320 | tf_op jit(solution)/shard_map/all_gather | solution.py:255
  583.8 6.4 copy.56
  590.2 15.3 %multiply_convert_fusion.12 = bf16[16,2048,128]{2,1,0:T(8,128)(2,1)S(1)} fusion(f32[16,2048,128]{2,1,0:T(8,128)} %fusion.105, f32[16,2048]{1,0:T(8,128)} %bitcast.183, f32[16,2048]{1,0:T(8,128)S(1)} %bitcast.181, pred[2048,128]{1,0:T(8,128)(4,1)S(1)} %copy-done.23, bf16[2048,16,64]{0,2,1:T(8,128)(2,1)} %bitcast.157, ...), kind=kOutput, calls=%fused_computation.clone.clone.clone.clone.1 | convolution fusion | flops 562036736 | bytes 30146560 | tf_op jit(solution)/shard_map/qhd,khd->hqk/dot_general | solution.py:269
  605.6 1.7 fusion.30
  608.6 11.1 fusion.34
  619.8 2.4 fusion.93
  622.2 1.1 fusion.94
  623.8 1.1 multiply_convert_fusion.4
  625.3 5.9 convolution_convert_fusion.1
  631.2 0.9 copy-done.13
  632.1 5.8 convolution_convert_fusion
  638.0 0.9 copy-done.19
  638.9 4.5 convolution_convert_fusion.2
  644.1 102.0 %reduce-scatter.10.cloned.1.call-done = bf16[512,4096]{1,0:T(8,128)(2,1)} async-done(((bf16[1024,4096]{1,0:T(8,128)(2,1)}), bf16[512,4096]{1,0:T(8,128)(2,1)}) %reduce-scatter.10.cloned.1.call-update) | async-done | bytes 4194320 | tf_op jit(solution)/shard_map/reduce_scatter | solution.py:300
  746.1 102.3 %reduce-scatter.12.cloned.1.call-done = bf16[2048,1024]{1,0:T(8,128)(2,1)} async-done(((bf16[4096,1024]{1,0:T(8,128)(2,1)}), bf16[2048,1024]{1,0:T(8,128)(2,1)}) %reduce-scatter.12.cloned.1.call-update) | async-done | bytes 4194320 | tf_op jit(solution)/shard_map/reduce_scatter | solution.py:303
  848.4 79.8 %reduce-scatter.6.cloned.1.call-done = bf16[512,3072]{1,0:T(8,128)(2,1)} async-done(((bf16[1024,3072]{1,0:T(8,128)(2,1)}), bf16[512,3072]{1,0:T(8,128)(2,1)}) %reduce-scatter.6.cloned.1.call-update) | async-done | bytes 3145744 | tf_op jit(solution)/shard_map/reduce_scatter | solution.py:294
  928.9 4.3 all-gather.4
  935.2 5.5 fusion.37
  940.7 7.1 all-reduce.15
  948.1 35.5 %all-reduce.13 = (bf16[512]{0:T(512)(128)(2,1)S(1)}, bf16[512]{0:T(512)(128)(2,1)S(1)}, bf16[512]{0:T(512)(128)(2,1)S(1)}, bf16[512]{0:T(512)(128)(2,1)S(1)}, bf...) all-reduce(bf16[512]{0:T(512)(128)(2,1)S(1)} %dynamic-slice.1, ...), channel_id=1, replica_groups=mesh['ctx'=16,'fsdp'=2] {'ctx'}, use_global_device_ids=true, to_apply=%region_23.24 | all-reduce | flops 4608 | bytes 18432 | tf_op jit(solution)/shard_map/psum | solution.py:347
  987.1 0.9 fusion.66
  988.0 191.3 %all-reduce.18.cloned.1.call-done = (bf16[512,3072]{1,0:T(8,128)(2,1)}, bf16[512,1024]{1,0:T(8,128)(2,1)}, bf16[512,4096]{1,0:T(8,128)(2,1)}, bf16[2048,1024]{1,0:T(8,128)(2,1)}, bf16[128,2048]{1,0:T(8,128)(2,1)}) async-done(((bf16[512,3072]{1,0:T(8,128)(2,1)}, bf16[512,1024]{1,0:T(8,128)(2,1)}, bf16[512,4096]{1,0:T(8,128)(2,1)}, bf16[2048,1024]{1,0:T(8,128)(2,1)}, bf16[128,2048]{1,0:T(8,128)(2,1)}), ...) | async-done | bytes 13107216 | tf_op jit(solution)/shard_map/psum | solution.py:342
  1179.3 5.5 convert_element_type.281
  1184.9 1.6 convert_element_type.283
  1186.4 4.5 convert_element_type.285
  1190.9 4.4 convert_element_type.287
  1195.4 1.1 convert_element_type.289
  (224 shorter events, 21.9 us)
Async XLA Ops:
  7.2 3.5 copy-start.55
  7.2 8.7 copy-start.56
  7.2 13.8 %copy-start.4 = (bf16[1,128,1024]{2,1,0:T(8,128)(2,1)S(1)}, bf16[1,128,1024]{2,1,0:T(8,128)(2,1)}, u32[]{:S(2)}) copy-start(bf16[1,128,1024]{2,1,0:T(8,128)(2,1)} %param.15) | copy-start | bytes 786436
  7.2 26.4 %all-gather.15.cloned.1.call-start = ((), (), s32[]{:S(2)}) async-start(), calls=%async_computation.5 | async-start | bytes 1572864 | tf_op jit(solution)/shard_map/all_gather | solution.py:104
  7.9 107.7 %all-gather.17.cloned.1.call-start = ((), (), s32[]{:S(2)}) async-start(), calls=%async_computation.6 | async-start | bytes 9437184 | tf_op jit(solution)/shard_map/all_gather | solution.py:100
  8.7 172.0 %all-gather.19.cloned.1.call-start = ((), (), s32[]{:S(2)}) async-start(), calls=%async_computation.7 | async-start | bytes 4456448 | tf_op jit(solution)/shard_map/all_gather | solution.py:157
  20.3 15.7 %copy-start.31 = (f32[2,1,512]{2,1,0:T(1,128)}, f32[2,1,512]{2,1,0:T(1,128)S(1)}, u32[]{:S(2)}) copy-start(f32[2,1,512]{2,1,0:T(1,128)S(1)} %convert_element_type.303) | copy-start | bytes 12292
  20.9 14.9 %copy-start.40 = (s32[128]{0:T(128)}, s32[128]{0:T(128)S(1)}, u32[]{:S(2)}) copy-start(s32[128]{0:T(128)S(1)} %get-tuple-element.44) | copy-start | bytes 1540
  21.1 98.3 %copy-start.47 = (f32[128]{0:T(128)}, f32[128]{0:T(128)S(1)}, u32[]{:S(2)}) copy-start(f32[128]{0:T(128)S(1)} %broadcast_multiply_fusion.1) | copy-start | bytes 1540
  21.3 98.1 %copy-start.53 = (f32[128]{0:T(128)}, f32[128]{0:T(128)S(1)}, u32[]{:S(2)}) copy-start(f32[128]{0:T(128)S(1)} %fusion.78) | copy-start | bytes 1540
  22.1 102.4 %copy-start.27 = (f32[128,32]{0,1:T(8,128)}, f32[128,32]{0,1:T(8,128)S(1)}, u32[]{:S(2)}) copy-start(f32[128,32]{0,1:T(8,128)S(1)} %get-tuple-element.65) | copy-start | bytes 49156
  127.3 104.7 %all-gather.21.cloned.1.call-start = ((), (), s32[]{:S(2)}) async-start(), calls=%async_computation.8 | async-start | bytes 4456448 | tf_op jit(solution)/shard_map/all_gather | solution.py:158
  128.1 137.0 %all-gather.23.cloned.1.call-start = ((), (), s32[]{:S(2)}) async-start(), calls=%async_computation.9 | async-start | bytes 3145728 | tf_op jit(solution)/shard_map/all_gather | solution.py:101
  128.7 241.8 %all-gather.25.cloned.1.call-start = ((), (), s32[]{:S(2)}) async-start(), calls=%async_computation.10 | async-start | bytes 12582912 | tf_op jit(solution)/shard_map/all_gather | solution.py:102
  129.3 5.8 copy-start.57
  129.3 10.1 copy-start.58
  129.3 14.5 %copy-start.41 = (s32[128]{0:T(128)S(1)}, s32[128]{0:T(128)}, u32[]{:S(2)}) copy-start(s32[128]{0:T(128)} %copy-done.40) | copy-start | bytes 1540
  129.3 14.7 %copy-start.21 = (bf16[128,16,1,32]{0,3,2,1:T(8,128)(2,1)S(1)}, bf16[128,16,1,32]{0,3,2,1:T(8,128)(2,1)}, u32[]{:S(2)}) copy-start(bf16[128,16,1,32]{0,3,2,1:T(8,128)(2,1)} %get-tuple-element.62) | copy-start | bytes 393220
  129.3 346.8 %all-gather.27.cloned.1.call-start = ((), (), s32[]{:S(2)}) async-start(), calls=%async_computation.11 | async-start | bytes 12582912 | tf_op jit(solution)/shard_map/all_gather | solution.py:103
  130.1 416.8 %all-gather.29.cloned.1.call-start = ((), (), s32[]{:S(2)}) async-start(), calls=%async_computation.12 | async-start | bytes 4456448 | tf_op jit(solution)/shard_map/all_gather | solution.py:254
  144.8 439.0 %all-gather.31.cloned.1.call-start = ((), (), s32[]{:S(2)}) async-start(), calls=%async_computation.13 | async-start | bytes 4456448 | tf_op jit(solution)/shard_map/all_gather | solution.py:255
  185.6 5.8 copy-start
  251.8 118.7 %copy-start.17 = (bf16[128,16,64]{0,2,1:T(8,128)(2,1)}, bf16[128,16,64]{0,2,1:T(8,128)(2,1)S(1)}, u32[]{:S(2)}) copy-start(bf16[128,16,64]{0,2,1:T(8,128)(2,1)S(1)} %get-tuple-element.69) | copy-start | bytes 786436
  251.8 118.7 %copy-start.33 = (f32[4096]{0:T(1024)S(1)}, f32[4096]{0:T(1024)}, u32[]{:S(2)}) copy-start(f32[4096]{0:T(1024)} %convert_element_type.264) | copy-start | bytes 49156
  267.2 223.2 %copy-start.36 = (f32[128]{0:T(128)}, f32[128]{0:T(128)S(1)}, u32[]{:S(2)}) copy-start(f32[128]{0:T(128)S(1)} %broadcast_multiply_fusion) | copy-start | bytes 1540
  267.4 223.0 %copy-start.38 = (f32[128]{0:T(128)}, f32[128]{0:T(128)S(1)}, u32[]{:S(2)}) copy-start(f32[128]{0:T(128)S(1)} %fusion.79) | copy-start | bytes 1540
  370.5 105.6 %copy-start.34 = (f32[128]{0:T(128)S(1)}, f32[128]{0:T(128)}, u32[]{:S(2)}) copy-start(f32[128]{0:T(128)} %get-tuple-element.43) | copy-start | bytes 1540
  476.1 10.7 copy-start.2
  486.8 3.5 copy-start.9
  486.8 4.6 copy-start.12
  490.4 2.6 copy-start.3
  490.7 3.9 copy-start.42
  490.7 5.5 copy-start.51
  494.5 149.1 %reduce-scatter.8.cloned.1.call-start = ((), (), s32[]{:S(2)}) async-start(), calls=%async_computation.15 | async-start | bytes 3145728 | tf_op jit(solution)/shard_map/reduce_scatter | solution.py:297
  571.6 18.6 %copy-start.23 = (pred[2048,128]{1,0:T(8,128)(4,1)S(1)}, pred[2048,128]{1,0:T(8,128)(4,1)}, u32[]{:S(2)}) copy-start(pred[2048,128]{1,0:T(8,128)(4,1)} %broadcast_compare_fusion) | copy-start | bytes 786436
  571.6 18.6 %copy-start.30 = (f32[2048,16]{0,1:T(8,128)S(1)}, f32[2048,16]{0,1:T(8,128)}, u32[]{:S(2)}) copy-start(f32[2048,16]{0,1:T(8,128)} %all_gather.71) | copy-start | bytes 393220
  571.6 72.5 %reduce-scatter.14.cloned.1.call-start = ((), (), s32[]{:S(2)}) async-start(), calls=%async_computation.18 | async-start | bytes 1572864 | tf_op jit(solution)/shard_map/reduce_scatter | solution.py:306
  590.2 15.3 %copy-start.1 = (bf16[2048,1024]{0,1:T(8,128)(2,1)S(1)}, bf16[2048,1024]{0,1:T(8,128)(2,1)}, u32[]{:S(2)}) copy-start(bf16[2048,1024]{0,1:T(8,128)(2,1)} %all-gather.29.cloned.1.call-done) | copy-start | bytes 12582916
  605.6 2.4 copy-start.11
  605.6 14.1 %slice-start = ((s8[6291456]{0:T(1024)(128)(4,1)}), s8[2097152]{0:T(1024)(128)(4,1)S(1)}, s32[]{:S(2)}) async-start(s8[6291456]{0:T(1024)(128)(4,1)} %bitcast.151), calls=%async_computation.20 | async-start | bytes 4194304
  608.5 11.2 copy-start.18
  608.5 11.2 slice-start.1
  608.6 11.2 copy-start.32
  608.6 11.2 copy-start.48
  619.7 2.5 copy-start.25
  619.8 2.4 copy-start.61
  619.8 2.4 copy-start.54
  623.3 2.0 copy-start.39
  625.0 121.2 %reduce-scatter.10.cloned.1.call-start = ((), (), s32[]{:S(2)}) async-start(), calls=%async_computation.16 | async-start | bytes 12582912 | tf_op jit(solution)/shard_map/reduce_scatter | solution.py:300
  631.2 217.2 %reduce-scatter.12.cloned.1.call-start = ((), (), s32[]{:S(2)}) async-start(), calls=%async_computation.17 | async-start | bytes 12582912 | tf_op jit(solution)/shard_map/reduce_scatter | solution.py:303
  637.9 290.3 %reduce-scatter.6.cloned.1.call-start = ((), (), s32[]{:S(2)}) async-start(), calls=%async_computation.14 | async-start | bytes 9437184 | tf_op jit(solution)/shard_map/reduce_scatter | solution.py:294
  643.5 535.8 %all-reduce.18.cloned.1.call-start = ((), (), s32[]{:S(2)}) async-start(), calls=%async_computation.19 | async-start | bytes 26214400 | tf_op jit(solution)/shard_map/psum | solution.py:342
  928.2 5.0 copy-start.63
  935.1 5.5 copy-start.43
  935.1 5.5 copy-start.44
  935.1 5.5 copy-start.45
  935.1 5.5 copy-start.46
  935.1 52.0 %copy-start.6 = (f32[128,1024]{1,0:T(8,128)S(1)}, f32[128,1024]{1,0:T(8,128)}, u32[]{:S(2)}) copy-start(f32[128,1024]{1,0:T(8,128)} %copy-done.5) | copy-start | bytes 1572868
  935.2 52.0 %copy-start.15 = (f32[128,1024]{1,0:T(8,128)S(1)}, f32[128,1024]{1,0:T(8,128)}, u32[]{:S(2)}) copy-start(f32[128,1024]{1,0:T(8,128)} %get-tuple-element.48) | copy-start | bytes 1572868
  935.2 52.0 %copy-start.52 = (f32[128]{0:T(128)S(1)}, f32[128]{0:T(128)}, u32[]{:S(2)}) copy-start(f32[128]{0:T(128)} %copy-done.51) | copy-start | bytes 1540
  1179.3 5.5 copy-start.16
  1179.3 7.1 copy-start.8
  1186.4 4.5 copy-start.7
  1190.9 4.4 copy-start.20
  (17 other events, 20.9 us)
Sparse Core Ops, SparseCore 0:
  9.6 23.9 all-gather.14
  35.2 80.4 all-gather.16
  127.4 53.2 all-gather.18
  183.3 48.7 all-gather.20
  233.4 31.5 all-gather.22
  266.5 103.9 all-gather.24
  372.0 103.9 all-gather.26
  478.8 53.9 all-gather.28
  535.0 48.7 all-gather.30
  586.4 30.2 reduce-scatter.7
  625.1 18.9 reduce-scatter.13
  646.8 99.2 reduce-scatter.9
  749.1 99.2 reduce-scatter.11
  851.1 77.0 reduce-scatter.5
  933.8 245.4 all-reduce.17
where the time goes:
time: 1210 us; the launch traced here: 1200 us
  waiting for transfers between devices  871 us (72%)
  matrix products  132 us (11%)
  blocking collectives  112 us (9%)
  other arithmetic  40 us (3%)
  local copies, waits for them, and re-layouts  29.2 us (2%)
  between operations  17.8 us (1%)
    psum x1, waiting for transfers between devices, body(): lax.psum(share_qkv.astype(jnp.bfloat16), 'ctx').astype(jnp.float32)  191 us
    all_gather x1, waiting for transfers between devices, body(): lax.all_gather(w_up, 'fsdp', axis=0, tiled=True)  103 us
    reduce_scatter x1, waiting for transfers between devices, body(): lax.psum_scatter(grad_down.astype(jnp.bfloat16), 'fsdp', scatter_dimensio...  102 us
    reduce_scatter x1, waiting for transfers between devices, body(): lax.psum_scatter(grad_up.astype(jnp.bfloat16), 'fsdp', scatter_dimension=...  102 us
    all_gather x1, waiting for transfers between devices, body(): lax.all_gather(w_down, 'fsdp', axis=0, tiled=True)  96.5 us
    reduce_scatter x1, waiting for transfers between devices, body(): lax.psum_scatter(grad_qkv.astype(jnp.bfloat16), 'fsdp', scatter_dimension...  79.8 us
    all_gather x1, waiting for transfers between devices, body(): lax.all_gather(w_qkv, 'fsdp', axis=0, tiled=True)  79.6 us
    all_gather x1, waiting for transfers between devices, body(): piece_values = lax.all_gather(value, 'ctx', axis=0, tiled=True)  40.6 us
  transfers between devices with their start and end apart: 15, of which 13 were waited for; matrix products, arithmetic and copies ran while one was open for 14% of the time, Pallas kernels for 0%

commit v1 on v0

v1 whole, which is shorter than its diff:
```python
import functools
import math

import jax
import jax.numpy as jnp
from jax import lax
from jax.experimental import pallas as pl
from jax.experimental.pallas import tpu as pltpu
from jax.sharding import PartitionSpec as P

HEADS = 16
EPSILON = 1e-05
NEGATIVE = -1e30
HIGH = lax.Precision.HIGHEST
F32 = jnp.float32
BF16 = jnp.bfloat16
VMEM_BYTES = 56 << 20


def dims(left, right, left_dim, right_dim):
    return lax.dot_general(
        left, right, (((left_dim,), (right_dim,)), ((), ())), preferred_element_type=F32
    )


def segments(ends, index):
    return sum((index >= end).astype(jnp.int32) for end in ends)


def positions(ends, index, segment):
    begin = jnp.zeros_like(index)
    for at, end in enumerate(ends):
        begin = jnp.where(segment > at, end, begin)
    return index - begin


def embed(steps_given, embed_width):
    half_width = embed_width // 2
    freq = jnp.exp(-math.log(10000.0) * jnp.arange(half_width, dtype=F32) / half_width)
    angle = steps_given.astype(F32)[..., None] * freq
    return jnp.concatenate([jnp.sin(angle), jnp.cos(angle)], axis=-1)


def stats(values):
    centre = jnp.mean(values, axis=-1, keepdims=True)
    centered = values - centre
    spread = jnp.mean(centered * centered, axis=-1, keepdims=True)
    scale = lax.rsqrt(spread + EPSILON)
    return centered * scale, scale


def stats_back(grad, normal, scale):
    return (
        grad
        - jnp.mean(grad, axis=-1, keepdims=True)
        - normal * jnp.mean(grad * normal, axis=-1, keepdims=True)
    ) * scale


def gelu_parts(pre):
    below = 0.5 * (1.0 + lax.erf(pre * math.sqrt(0.5)))
    density = jnp.exp(-0.5 * pre * pre) * (1.0 / math.sqrt(2.0 * math.pi))
    return pre * below, below + pre * density


def qkv_kernel(
    rows, head_size, ends_ref, base_ref, tokens_ref, gains_ref, shifts_ref, w_ref,
    cos_ref, sin_ref, norm_ref, query_t_ref, key_ref, key_t_ref, value_t_ref, pair_ref,
):
    step = pl.program_id(0)
    block = tokens_ref.shape[0]
    seq_count = ends_ref.shape[0]
    half = head_size // 2
    values = tokens_ref[...].astype(F32)
    normal, _ = stats(values)
    chunks = block // rows

    def token_index(shape, axis):
        within = lax.broadcasted_iota(jnp.int32, shape, axis)
        index = within + base_ref[step * chunks]
        for at in range(1, chunks):
            index = jnp.where(
                within >= at * rows,
                within - at * rows + base_ref[step * chunks + at],
                index,
            )
        return index

    ends = [ends_ref[s] for s in range(seq_count)]
    seg_col = segments(ends, token_index((block, 1), 0))
    seg_row = segments(ends, token_index((1, block), 1))
    gains = gains_ref[0:1, :]
    shifts = shifts_ref[0:1, :]
    for s in range(1, seq_count + 1):
        gains = jnp.where(seg_col == s, gains_ref[s : s + 1, :], gains)
        shifts = jnp.where(seg_col == s, shifts_ref[s : s + 1, :], shifts)
    norm = (normal * gains + shifts).astype(BF16)
    norm_ref[...] = norm
    mixed = jnp.dot(norm, w_ref[...], preferred_element_type=F32)
    turned = mixed.T
    cos = cos_ref[...]
    sin = sin_ref[...]

    def turn(at):
        upper = turned[at : at + half]
        lower = turned[at + half : at + head_size]
        return jnp.concatenate(
            [upper * cos - lower * sin, lower * cos + upper * sin], axis=0
        ).astype(BF16)

    query = turn(0).astype(F32) * (float(head_size) ** -0.5)
    key = turn(head_size).astype(F32)
    value = turned[2 * head_size : 3 * head_size].astype(BF16).astype(F32)
    spare = 128 - head_size
    row_id = lax.broadcasted_iota(jnp.int32, (spare, block), 0)
    same = row_id == seg_row
    used = row_id <= seq_count
    key_tail = jnp.where(same & used, 1.0, 0.0)
    query_tail = jnp.where(used & jnp.logical_not(same), NEGATIVE, 0.0)
    query_t_ref[...] = jnp.concatenate([query, query_tail], axis=0).astype(BF16)
    key_t_ref[...] = key.astype(BF16)
    value_t_ref[...] = value.astype(BF16)
    key_ref[...] = jnp.concatenate([key, key_tail], axis=0).T.astype(BF16)
    pair_ref[...] = jnp.concatenate([value, query], axis=0).T.astype(BF16)


def attend_kernel(chunk, rows, query_ref, key_ref, value_ref, out_ref, sent_ref, lse_ref, score_ref):
    count = key_ref.shape[0]
    query = query_ref[...]
    top = None
    for at in range(0, count, chunk):
        score = jnp.dot(key_ref[at : at + chunk, :], query, preferred_element_type=F32)
        score_ref[at : at + chunk, :] = score
        high = jnp.max(score, axis=0, keepdims=True)
        top = high if top is None else jnp.maximum(top, high)
    total = jnp.zeros_like(top)
    out = jnp.zeros(out_ref.shape, F32)
    for at in range(0, count, chunk):
        weight = jnp.exp(score_ref[at : at + chunk, :] - top)
        total = total + jnp.sum(weight, axis=0, keepdims=True)
        out = out + jnp.dot(
            value_ref[:, at : at + chunk],
            weight.astype(BF16),
            preferred_element_type=F32,
        )
    out = out / total
    out_ref[...] = out
    for at in range(sent_ref.shape[0]):
        sent_ref[at] = out[:, at * rows : (at + 1) * rows].astype(BF16)
    lse_ref[...] = top + jnp.log(total)


def attend_back_kernel(
    chunk, rows, head_size, query_ref, grad_ref, out_ref, lse_ref, key_ref, key_t_ref, pair_ref,
    pair_block_ref, cos_block_ref, sin_block_ref, cos_ref, sin_ref, mixed_ref, key_acc, value_acc,
):
    step = pl.program_id(0)
    count = key_ref.shape[0]
    block = query_ref.shape[1]
    half = head_size // 2
    scale = float(head_size) ** -0.5

    @pl.when(step == 0)
    def _():
        key_acc[...] = jnp.zeros_like(key_acc)
        value_acc[...] = jnp.zeros_like(value_acc)

    query = query_ref[...]
    grad = jnp.concatenate(
        [grad_ref[at] for at in range(grad_ref.shape[0])], axis=1
    ).astype(F32)
    delta = jnp.sum(grad * out_ref[...], axis=0, keepdims=True)
    lse = lse_ref[...]
    grad_t = jnp.concatenate(
        [grad, jnp.zeros((128 - head_size, block), F32)], axis=0
    )
    grad_rows = grad_t.T.astype(BF16)
    grad_t = grad_t.astype(BF16)
    pair = pair_block_ref[...]
    grad_query = jnp.zeros((head_size, block), F32)
    for at in range(0, count, chunk):
        part = slice(at, at + chunk)
        score = jnp.dot(key_ref[part, :], query, preferred_element_type=F32)
        prob = jnp.exp(score - lse)
        grad_prob = jnp.dot(pair_ref[part, :], grad_t, preferred_element_type=F32)
        grad_score = (prob * (grad_prob - delta)).astype(BF16)
        grad_query = grad_query + jnp.dot(
            key_t_ref[:, part], grad_score, preferred_element_type=F32
        )
        key_acc[part, :] += jnp.dot(grad_score, pair, preferred_element_type=F32)
        value_acc[part, :] += jnp.dot(
            prob.astype(BF16), grad_rows, preferred_element_type=F32
        )

    def turn_back(values, cos, sin):
        upper = values[:half]
        lower = values[half:]
        return jnp.concatenate(
            [upper * cos + lower * sin, lower * cos - upper * sin], axis=0
        ).astype(BF16)

    at = pl.multiple_of(step * block, block)
    mixed_ref[0:head_size, pl.ds(at, block)] = turn_back(
        grad_query * scale, cos_block_ref[...], sin_block_ref[...]
    )

    @pl.when(step == pl.num_programs(0) - 1)
    def _():
        mixed_ref[head_size : 2 * head_size, :] = turn_back(
            key_acc[...].T[head_size : 2 * head_size], cos_ref[...], sin_ref[...]
        )
        mixed_ref[2 * head_size : 3 * head_size, :] = value_acc[...].T[
            :head_size
        ].astype(BF16)


def whole(shape):
    return pl.BlockSpec(shape, lambda i, *_: (0,) * len(shape))


def project(tokens, base, ends, gains, shifts, w_head, cos, sin, rows, head_size):
    count, width = tokens.shape
    block = min(count, 2 * rows)
    grid_spec = pltpu.PrefetchScalarGridSpec(
        num_scalar_prefetch=2,
        grid=(count // block,),
        in_specs=[
            pl.BlockSpec((block, width), lambda i, *_: (i, 0)),
            whole(gains.shape),
            whole(shifts.shape),
            whole(w_head.shape),
            pl.BlockSpec((head_size // 2, block), lambda i, *_: (0, i)),
            pl.BlockSpec((head_size // 2, block), lambda i, *_: (0, i)),
        ],
        out_specs=[
            pl.BlockSpec((block, width), lambda i, *_: (i, 0)),
            pl.BlockSpec((128, block), lambda i, *_: (0, i)),
            pl.BlockSpec((block, 128), lambda i, *_: (i, 0)),
            pl.BlockSpec((head_size, block), lambda i, *_: (0, i)),
            pl.BlockSpec((head_size, block), lambda i, *_: (0, i)),
            pl.BlockSpec((block, 128), lambda i, *_: (i, 0)),
        ],
    )
    return pl.pallas_call(
        functools.partial(qkv_kernel, rows, head_size),
        grid_spec=grid_spec,
        out_shape=[
            jax.ShapeDtypeStruct((count, width), BF16),
            jax.ShapeDtypeStruct((128, count), BF16),
            jax.ShapeDtypeStruct((count, 128), BF16),
            jax.ShapeDtypeStruct((head_size, count), BF16),
            jax.ShapeDtypeStruct((head_size, count), BF16),
            jax.ShapeDtypeStruct((count, 128), BF16),
        ],
        compiler_params=pltpu.CompilerParams(vmem_limit_bytes=VMEM_BYTES),
        cost_estimate=pl.CostEstimate(
            flops=2 * count * width * 256,
            bytes_accessed=4 * count * width,
            transcendentals=0,
        ),
        name="project_head",
    )(ends, base, tokens, gains, shifts, w_head, cos, sin)


def attend(query_t, key, value_t, rows):
    count = key.shape[0]
    head_size = value_t.shape[0]
    block = min(count, 2 * rows)
    chunk = min(count, 512)
    return pl.pallas_call(
        functools.partial(attend_kernel, chunk, rows),
        grid=(count // block,),
        in_specs=[
            pl.BlockSpec((128, block), lambda i: (0, i)),
            whole((count, 128)),
            whole((head_size, count)),
        ],
        out_specs=[
            pl.BlockSpec((head_size, block), lambda i: (0, i)),
            pl.BlockSpec((block // rows, head_size, rows), lambda i: (i, 0, 0)),
            pl.BlockSpec((1, block), lambda i: (0, i)),
        ],
        out_shape=[
            jax.ShapeDtypeStruct((head_size, count), F32),
            jax.ShapeDtypeStruct((count // rows, head_size, rows), BF16),
            jax.ShapeDtypeStruct((1, count), F32),
        ],
        scratch_shapes=[pltpu.VMEM((count, block), F32)],
        compiler_params=pltpu.CompilerParams(vmem_limit_bytes=VMEM_BYTES),
        cost_estimate=pl.CostEstimate(
            flops=8 * count * count * 128,
            bytes_accessed=8 * count * 128,
            transcendentals=count * count,
        ),
        name="attend_head",
    )(query_t, key, value_t)


def attend_back(query_t, grad, out, lse, key, key_t, pair, cos, sin, rows):
    count = key.shape[0]
    head_size = key_t.shape[0]
    half = head_size // 2
    block = min(count, 2 * rows)
    chunk = min(count, 512)
    return pl.pallas_call(
        functools.partial(attend_back_kernel, chunk, rows, head_size),
        grid=(count // block,),
        in_specs=[
            pl.BlockSpec((128, block), lambda i: (0, i)),
            pl.BlockSpec((block // rows, head_size, rows), lambda i: (i, 0, 0)),
            pl.BlockSpec((head_size, block), lambda i: (0, i)),
            pl.BlockSpec((1, block), lambda i: (0, i)),
            whole((count, 128)),
            whole((head_size, count)),
            whole((count, 128)),
            pl.BlockSpec((block, 128), lambda i: (i, 0)),
            pl.BlockSpec((half, block), lambda i: (0, i)),
            pl.BlockSpec((half, block), lambda i: (0, i)),
            whole((half, count)),
            whole((half, count)),
        ],
        out_specs=whole((3 * head_size, count)),
        out_shape=jax.ShapeDtypeStruct((3 * head_size, count), BF16),
        scratch_shapes=[pltpu.VMEM((count, 128), F32), pltpu.VMEM((count, 128), F32)],
        compiler_params=pltpu.CompilerParams(vmem_limit_bytes=VMEM_BYTES),
        cost_estimate=pl.CostEstimate(
            flops=20 * count * count * 128,
            bytes_accessed=16 * count * 128,
            transcendentals=count * count,
        ),
        name="attend_head_back",
    )(query_t, grad, out, lse, key, key_t, pair, pair, cos, sin, cos, sin)


def times_rows(values, pieces):
    return sum(
        jnp.dot(
            lax.dynamic_slice_in_dim(values, at, piece.shape[0], 1),
            piece,
            preferred_element_type=F32,
        )
        for piece, at in pieces
    )


def times_rows_t(values_t, pieces):
    return sum(
        dims(lax.dynamic_slice_in_dim(values_t, at, piece.shape[0], 0), piece, 0, 0)
        for piece, at in pieces
    )


def joined(parts, pieces, dim):
    if len(parts) == 1:
        return parts[0]
    shape = list(parts[0].shape)
    shape[dim] = sum(part.shape[dim] for part in parts)
    out = jnp.zeros(shape, parts[0].dtype)
    for part, (_, at) in zip(parts, pieces):
        out = lax.dynamic_update_slice_in_dim(out, part, at, dim)
    return out


def rows_of(pieces, start, size):
    out = None
    for piece, at in pieces:
        length = piece.shape[0]
        local = jnp.clip(start - at, 0, length - size)
        found = lax.dynamic_slice_in_dim(piece, local, size, 0)
        inside = (start >= at) & (start < at + length)
        out = found if out is None else jnp.where(inside, found, out)
    return out


def body(
    ctx_size, fsdp_size,
    tokens, w_qkv, w_out, w_up, w_down, w_time, gain_one, bias_one, gain_two, bias_two, bias_up,
    bias_down, lengths, time_steps, cotangent,
):
    me = lax.axis_index("ctx")
    shard = lax.axis_index("fsdp")
    core = me % 2
    rows = tokens.shape[1]
    width = tokens.shape[2]
    count = rows * ctx_size
    head_size = width // HEADS
    repeats = ctx_size // HEADS
    columns = head_size // repeats
    seq_count = lengths.shape[1]
    hidden = w_up.shape[1]
    paired = fsdp_size == 2

    def across(values):
        return lax.ppermute(values, "fsdp", [(0, 1), (1, 0)])

    def core_swap(values):
        return lax.ppermute(values, "ctx", [(i, i ^ 1) for i in range(ctx_size)])

    def gather_small(values):
        if not paired:
            return lax.all_gather(values, "fsdp", axis=0, tiled=True)
        other = across(values)
        first = jnp.where(shard == 0, values, other)
        second = jnp.where(shard == 0, other, values)
        return jnp.concatenate([first, second], axis=0)

    def fetch(weight):
        if not paired:
            return [(lax.all_gather(weight, "fsdp", axis=0, tiled=True), 0)]
        size = weight.shape[0]
        half = size // 2
        mine = across(lax.dynamic_slice_in_dim(weight, core * half, half, 0))
        theirs = core_swap(mine)
        other = (1 - shard) * size
        return [
            (weight, shard * size),
            (mine, other + core * half),
            (theirs, other + (1 - core) * half),
        ]

    def scatter_sum(values, dim):
        if not paired:
            return lax.psum_scatter(
                values.astype(BF16), "fsdp", scatter_dimension=dim, tiled=True
            )
        half = values.shape[dim] // 2
        keep = lax.dynamic_slice_in_dim(values, shard * half, half, dim)
        send = lax.dynamic_slice_in_dim(values, (1 - shard) * half, half, dim)
        return (keep + across(send.astype(BF16)).astype(F32)).astype(BF16)

    def gather(values):
        return lax.all_gather(values, "ctx", axis=0, tiled=False)

    ends = []
    for s in range(seq_count):
        ends.append(lengths[0, s] + (ends[-1] if ends else 0))
    ends_vector = jnp.stack(ends)
    index = me * rows + jnp.arange(rows, dtype=jnp.int32)
    segment = segments(ends, index)
    live = (segment < seq_count).astype(F32)[:, None]
    all_index = jnp.arange(count, dtype=jnp.int32)
    all_position = positions(ends, all_index, segments(ends, all_index))
    half_width = head_size // 2
    inverse = jnp.exp(
        -math.log(10000.0) * jnp.arange(half_width, dtype=F32) / half_width
    )
    angle = inverse[:, None] * all_position.astype(F32)[None, :]
    cos = jnp.cos(angle)
    sin = jnp.sin(angle)

    all_tokens = gather(tokens[0]).reshape(count, width)
    inputs = tokens[0].astype(F32)
    grad_y = cotangent[0].astype(F32) * live
    grad_y_b = grad_y.astype(BF16)
    all_grad_y = gather(grad_y_b).reshape(count, width)

    small = [gain_one, bias_one, gain_two, bias_two, bias_down, bias_up]
    packed = gather_small(jnp.concatenate(small)[None, :])
    vectors = []
    at = 0
    for vector in small:
        size = vector.shape[0]
        vectors.append(packed[:, at : at + size].reshape(1, -1).astype(F32))
        at += size
    gain_first, bias_first, gain_second, bias_second, bias_output, bias_hidden = vectors

    all_steps = lax.all_gather(time_steps.astype(F32), "fsdp", axis=0, tiled=True)
    all_embedded = embed(all_steps, w_time.shape[0] * fsdp_size).astype(BF16)
    embedded = lax.dynamic_index_in_dim(all_embedded, shard, 0, keepdims=False)
    film = times_rows(embedded, fetch(w_time))
    film = jnp.concatenate([film, jnp.zeros((1, 2 * width), F32)], axis=0)
    gains = gain_first + film[:, :width]
    shifts = bias_first + film[:, width:]

    head = me // repeats
    w_head = jnp.concatenate(
        [
            lax.dynamic_slice_in_dim(w_qkv, k * width + head * head_size, head_size, 1)
            for k in range(3)
        ]
        + [jnp.zeros((w_qkv.shape[0], head_size), BF16)],
        axis=1,
    )
    w_head = gather_small(w_head)

    base = jnp.arange(ctx_size, dtype=jnp.int32) * rows
    all_norm, query_t, key, key_t, value_t, pair = project(
        all_tokens, base, ends_vector, gains, shifts, w_head, cos, sin, rows, head_size
    )
    out_t, sent, lse = attend(query_t, key, value_t, rows)

    part = (me % repeats) * columns
    if repeats > 1:
        sent = lax.dynamic_slice_in_dim(sent, part, columns, 1)
    attended_t = lax.all_to_all(sent, "ctx", 0, 0, tiled=True).reshape(width, rows)

    out_pieces = fetch(w_out)
    up_pieces = fetch(w_up)
    down_pieces = fetch(w_down)
    qkv_pieces = fetch(w_qkv)
    resid = inputs + times_rows_t(attended_t, out_pieces)
    normal_two, scale_two = stats(resid)
    norm_two_b = (normal_two * gain_second + bias_second).astype(BF16)
    all_norm_two = gather(norm_two_b).reshape(count, width)
    pre = times_rows(norm_two_b, up_pieces) + bias_hidden
    act, slope = gelu_parts(pre)
    branch = times_rows(act.astype(BF16), down_pieces) + bias_output
    output = (live * (resid + branch)).astype(BF16)
    grad_act = joined([dims(grad_y_b, p, 1, 1) for p, _ in down_pieces], down_pieces, 1)
    grad_pre = grad_act * slope
    grad_bias_up = jnp.sum(grad_pre, axis=0)
    grad_pre_b = grad_pre.astype(BF16)
    grad_norm_two = joined([dims(grad_pre_b, p, 1, 1) for p, _ in up_pieces], up_pieces, 1)
    grad_resid = grad_y + stats_back(grad_norm_two * gain_second, normal_two, scale_two)
    grad_resid_b = grad_resid.astype(BF16)
    grad_att_t = joined(
        [dims(p, grad_resid_b, 1, 1) for p, _ in out_pieces], out_pieces, 0
    ).astype(BF16)
    grad_att_t = grad_att_t.reshape(HEADS, head_size, rows)
    if repeats > 1:
        grad_att_t = jnp.repeat(grad_att_t, repeats, axis=0)
    grad_att = lax.all_to_all(grad_att_t, "ctx", 0, 0, tiled=True)

    mixed_t = attend_back(
        query_t, grad_att, out_t, lse, key, key_t, pair, cos, sin, rows
    )
    mixed_t = mixed_t.reshape(3, head_size, count)
    if repeats > 1:
        mixed_t = lax.dynamic_slice_in_dim(mixed_t, part, columns, 1)
    mixed_t = mixed_t.reshape(3 * columns, count)
    mixed_sent = mixed_t.reshape(3 * columns, ctx_size, rows).transpose(1, 0, 2)
    mixed_got = lax.all_to_all(mixed_sent, "ctx", 0, 0, tiled=True)
    grad_mixed_t = (
        mixed_got.reshape(ctx_size, 3, columns, rows)
        .transpose(1, 0, 2, 3)
        .reshape(3 * width, rows)
    )
    grad_norm_one = joined(
        [dims(grad_mixed_t, p, 0, 1) for p, _ in qkv_pieces], qkv_pieces, 1
    )
    normal_one, scale_one = stats(inputs)
    seg_col = segment[:, None]
    gain_tok = gains[0:1]
    for s in range(1, seq_count + 1):
        gain_tok = jnp.where(seg_col == s, gains[s : s + 1], gain_tok)
    grad_tokens = (
        grad_resid + stats_back(grad_norm_one * gain_tok, normal_one, scale_one)
    ).astype(BF16)
    film_terms = jnp.concatenate([grad_norm_one * normal_one, grad_norm_one], axis=1)
    film_sums = [
        jnp.sum(jnp.where(seg_col == s, film_terms, 0.0), axis=0)
        for s in range(seq_count + 1)
    ]

    sums = [
        jnp.sum(grad_norm_two * normal_two, axis=0),
        jnp.sum(grad_norm_two, axis=0),
        jnp.sum(grad_y, axis=0),
        grad_bias_up,
    ] + film_sums
    sizes = [vector.shape[0] for vector in sums]
    total = lax.psum(jnp.concatenate(sums)[None, :], "ctx")
    total = lax.all_gather(total, "fsdp", axis=0, tiled=True)
    split = []
    at = 0
    for size in sizes:
        split.append(total[:, at : at + size])
        at += size

    def own(vector):
        size = vector.shape[0] // fsdp_size
        return lax.dynamic_slice_in_dim(vector, shard * size, size, 0)

    sum_gain_two, sum_bias_two, sum_bias_down, sum_bias_up = (
        own(jnp.sum(vector, axis=0)) for vector in split[:4]
    )
    film_all = jnp.sum(sum(split[4:]), axis=0)
    sum_gain_one = own(film_all[:width])
    sum_bias_one = own(film_all[width:])
    film_grad = jnp.stack(split[4 : 4 + seq_count], axis=1).reshape(-1, 2 * width)
    embedded_rows = lax.dynamic_slice_in_dim(
        all_embedded.astype(F32).reshape(film_grad.shape[0], -1),
        shard * w_time.shape[0],
        w_time.shape[0],
        1,
    )
    grad_time = sum(
        embedded_rows[g][:, None] * film_grad[g][None, :]
        for g in range(film_grad.shape[0])
    )

    slice_width = hidden // (ctx_size * fsdp_size)
    starts = [
        k * (hidden // fsdp_size) + me * slice_width for k in range(fsdp_size)
    ]
    w_up_cols = []
    for piece, _ in up_pieces:
        w_up_cols.append(
            jnp.concatenate(
                [
                    lax.dynamic_slice_in_dim(piece, start, slice_width, 1)
                    for start in starts
                ],
                axis=1,
            )
        )
    w_up_slice = joined(w_up_cols, up_pieces, 0)
    w_down_slice = jnp.concatenate(
        [rows_of(down_pieces, start, slice_width) for start in starts], axis=0
    )
    bias_slice = jnp.concatenate(
        [
            lax.dynamic_slice_in_dim(bias_hidden, start, slice_width, 1)
            for start in starts
        ],
        axis=1,
    )
    pre_slice = dims(all_norm_two, w_up_slice, 1, 0) + bias_slice
    act_slice, slope_slice = gelu_parts(pre_slice)
    grad_pre_slice = (dims(all_grad_y, w_down_slice, 1, 1) * slope_slice).astype(BF16)
    down_slice = dims(act_slice.astype(BF16), all_grad_y, 0, 0)
    up_slice = dims(all_norm_two, grad_pre_slice, 0, 0)
    grad_down = gather(scatter_sum(down_slice, 0)).reshape(-1, width).astype(F32)
    up_parts = gather(scatter_sum(up_slice, 0))
    grad_up = (
        up_parts.reshape(ctx_size, width // fsdp_size, fsdp_size, slice_width)
        .transpose(1, 2, 0, 3)
        .reshape(width // fsdp_size, hidden)
        .astype(F32)
    )
    out_part = jnp.dot(attended_t, grad_resid_b, preferred_element_type=F32)
    out_rows = lax.psum_scatter(
        out_part.astype(BF16), ("fsdp", "ctx"), scatter_dimension=0, tiled=True
    )
    grad_out = gather(out_rows).reshape(-1, width).astype(F32)
    qkv_slice = jnp.dot(mixed_t, all_norm, preferred_element_type=F32)
    qkv_parts = gather(scatter_sum(qkv_slice, 1))
    grad_qkv = (
        qkv_parts.reshape(ctx_size, 3, columns, width // fsdp_size)
        .transpose(3, 1, 0, 2)
        .reshape(width // fsdp_size, 3 * width)
        .astype(F32)
    )
    return (
        output[None],
        grad_tokens[None],
        grad_qkv,
        grad_out,
        grad_up,
        grad_down,
        grad_time,
        sum_gain_one,
        sum_bias_one,
        sum_gain_two,
        sum_bias_two,
        sum_bias_up,
        sum_bias_down,
    )


def solution(mesh):
    in_specs = (
        (P("fsdp", "ctx", None),)
        + (P("fsdp", None),) * 5
        + (P("fsdp"),) * 6
        + (P("fsdp", None), P("fsdp", None), P("fsdp", "ctx", None))
    )
    out_specs = (
        (P("fsdp", "ctx", None),) * 2 + (P("fsdp", None),) * 5 + (P("fsdp"),) * 6
    )
    return jax.shard_map(
        functools.partial(body, mesh.shape["ctx"], mesh.shape["fsdp"]),
        mesh=mesh,
        in_specs=in_specs,
        out_specs=out_specs,
        check_vma=False,
    )
```

time: 1210 us -> 667 us (0.55)
  waiting for transfers between devices: 871 us -> 278 us
  matrix products: 132 us -> 75.1 us
  local copies, waits for them, and re-layouts: 29.2 us -> 72.9 us
  Pallas kernels: 0 us -> 40.4 us
  starting transfers between devices: 1.32 us -> 28.8 us
  other arithmetic: 40 us -> 27.5 us
    all_gather x9 -> x7, waiting for transfers between devices: 392 us -> 63.6 us  [gather(): return lax.all_gather(values, 'ctx', axis=0, tiled=False)]
    psum x1 -> x0, waiting for transfers between devices: 191 us -> none  [body(): lax.psum(share_qkv.astype(jnp.bfloat16), 'ctx').astype(jnp.float32)]
    reduce_scatter x5 -> x1, waiting for transfers between devices: 285 us -> 124 us  [body(): lax.psum_scatter(out_part.astype(BF16), ('fsdp', 'ctx'), scatter_dimensio...]
    ppermute x0 -> x15, waiting for transfers between devices: none -> 83.8 us  [the longest x10 83.8 us: across(): return lax.ppermute(values, 'fsdp', [(0, 1), (1, 0)])]
    all_gather x8 -> x1, blocking collectives: 69.7 us -> 4.71 us  [body(): total = lax.all_gather(total, 'fsdp', axis=0, tiled=True)]
    dot_general x22 -> x29, matrix products: 132 us -> 75.1 us  [the longest x18 49.3 us: dims(): lax.dot_general(left, right, (((left_dim,), (right_dim,)), ((), ())), pre...]
    unnamed x1, blocking collectives: 7.08 us -> 55.6 us
    pallas_call x0 -> x3, Pallas kernels: none -> 40.4 us  [the longest x1 17.8 us: attend_back(): pl.pallas_call(functools.partial(attend_back_kernel, chunk, rows, head_si...]
  transfers between devices with their start and end apart: 15 -> 26, of which waited for: 13 -> 9; matrix products, arithmetic and copies ran while one was open for 14% -> 23% of each run, Pallas kernels for 0% -> 6%
where the time goes in v1:
time: 667 us; the launch traced here: 659 us
  waiting for transfers between devices  278 us (42%)
  blocking collectives  120 us (18%)
  matrix products  75.1 us (11%)
  local copies, waits for them, and re-layouts  72.9 us (11%)
  Pallas kernels  40.4 us (6%)
  starting transfers between devices  28.8 us (4%)
  other arithmetic  27.5 us (4%)
  between operations  16.6 us (2%)
    reduce_scatter x1, waiting for transfers between devices, body(): lax.psum_scatter(out_part.astype(BF16), ('fsdp', 'ctx'), scatter_dimensio...  124 us
    ppermute x10, waiting for transfers between devices, across(): return lax.ppermute(values, 'fsdp', [(0, 1), (1, 0)])  83.8 us
    all_gather x7, waiting for transfers between devices, gather(): return lax.all_gather(values, 'ctx', axis=0, tiled=False)  63.6 us
    psum x1, blocking collectives, body(): total = lax.psum(jnp.concatenate(sums)[None, :], 'ctx')  59.8 us
    unnamed x1, blocking collectives  55.6 us
    dot_general x18, matrix products, dims(): lax.dot_general(left, right, (((left_dim,), (right_dim,)), ((), ())), pre...  49.3 us
    unnamed x77, local copies, waits for them, and re-layouts  26 us
    dot_general x9, matrix products, times_rows(): jnp.dot(lax.dynamic_slice_in_dim(values, at, piece.shape[0], 1), piece, p...  20.7 us
  transfers between devices with their start and end apart: 26, of which 9 were waited for; matrix products, arithmetic and copies ran while one was open for 23% of the time, Pallas kernels for 6%

profile of v1, /device:TPU:0, one launch (start us, length us, event | category | flops | bytes accessed | tf_op | source)
XLA Modules:
  0.0 659.3 jit_solution(12165848608948817824)
XLA Ops:
  8.0 1.7 constant_dynamic-slice_fusion.21
  9.6 2.9 collective-permute-start.1
  21.2 2.0 collective-permute-start.3
  26.0 1.8 constant_dynamic-slice_fusion.14
  27.8 2.1 collective-permute-start.8
  29.8 55.6 %all-reduce.1 = f32[2]{0:T(128)S(1)} all-reduce(f32[2]{0:T(128)S(1)} %bitcast_dynamic-update-slice_fusion), channel_id=1, replica_groups=mesh['ctx'=16,'fsdp'=2] {'fsdp'}, use_global_device_ids=true, to_apply=%add.1 | all-reduce | flops 2 | bytes 16
  86.3 1.9 fusion.74
  88.2 1.8 multiply_sine_fusion
  90.0 3.1 constant_dynamic-slice_fusion.15
  93.1 1.5 broadcast_in_dim.90
  94.7 4.7 convolution_dynamic-update-slice_fusion
  99.9 1.7 collective-permute-start.6
  104.8 1.3 broadcast_select_fusion.1
  109.7 36.7 %collective-permute-done.6 = bf16[256,4096]{1,0:T(8,128)(2,1)} collective-permute-done((bf16[256,4096]{1,0:T(8,128)(2,1)}, bf16[256,4096]{1,0:T(8,128)(2,1)}, u32[]{:S(2)}, u32[]{:S(2)}) %collective-permute-start.6) | collective-permute-done | bytes 2097184 | tf_op jit(solution)/shard_map/ppermute | solution.py:394
  146.4 10.5 %project_head.1 = (bf16[2048,1024]{1,0:T(8,128)(2,1)}, bf16[128,2048]{1,0:T(8,128)(2,1)}, bf16[2048,128]{1,0:T(8,128)(2,1)}, bf16[64,2048]{1,0:T(8,128)(2,1)}, b...) custom-call(s32[1]{0:T(128)} %bitcast.185.ends_ref, s32[16]{0:T(128)} %iota_multiply_fusion.base_ref, ...), custom_call_target="tpu_custom_call" | custom-call | flops 1073741824 | bytes 8388608 | tf_op jit(solution)/shard_map/project_head/pallas_call | solution.py:244
  157.0 12.1 %attend_head.1 = (f32[64,2048]{1,0:T(8,128)}, bf16[16,64,128]{2,1,0:T(8,128)(2,1)}, f32[1,2048]{1,0:T(1,128)}) custom-call(bf16[128,2048]{1,0:T(8,128)(2,1)} %get-tuple-element.22.query_ref, bf16[2048,128]{1,0:T(8,128)(2,1)} %get-tuple-element.23.key_ref, bf16[64,2048]{1,0:T(8,128)(2,1)} %get-tuple-element.24.value_ref), custom_call_target="tpu_custom_call" | custom-call | flops 4294967296 | bytes 2097152 | tf_op jit(solution)/shard_map/attend_head/pallas_call | solution.py:270
  169.0 6.0 all-to-all-start
  175.3 3.2 convolution_dynamic-update-slice_fusion.2
  178.6 1.6 convolution_dynamic-update-slice_fusion.1
  180.2 5.0 all-to-all-done
  186.4 1.3 convolution_add_fusion.6
  187.8 1.4 fusion.112
  189.6 3.0 fusion.48
  192.6 2.1 convolution_add_fusion.1
  194.8 4.7 fusion.105
  199.6 1.5 convolution_dynamic-update-slice_fusion.4
  201.1 2.5 convolution_dynamic-update-slice_fusion.10
  203.6 2.5 convolution_dynamic-update-slice_fusion.9
  207.5 3.0 convolution_convert_fusion
  214.1 2.0 convolution_dynamic-update-slice_fusion.8
  216.1 2.0 convolution_dynamic-update-slice_fusion.7
  218.1 3.5 all-to-all-start.1
  221.7 124.1 %reduce-scatter.2.cloned.1.call-done = bf16[32,1024]{1,0:T(8,128)(2,1)} async-done(((bf16[1024,1024]{1,0:T(8,128)(2,1)}), bf16[32,1024]{1,0:T(8,128)(2,1)}) %reduce-scatter.2.cloned.1.call-update) | async-done | bytes 65552 | tf_op jit(solution)/shard_map/reduce_scatter | solution.py:632
  346.6 17.8 %attend_head_back.1 = bf16[192,2048]{1,0:T(8,128)(2,1)} custom-call(bf16[128,2048]{1,0:T(8,128)(2,1)} %get-tuple-element.22.query_ref, bf16[16,64,128]{2,1,0:T(8,128)(2,1)} %copy-done.15, f32[64,2048]{1,0:T(8,128)} %get-tuple-element.26.out_ref, f32[1,2048]{1,0:T(1,128)} %get-tuple-element.27.lse_ref, bf16[2048,128]{1,0:T(8,128)(2,1)} %get-tuple-element.23.key_ref, ...), custom_call_target="tpu_custom_call" | custom-call | flops 10737418240 | bytes 4194304 | tf_op jit(solution)/shard_map/attend_head_back/pallas_call | solution.py:305
  364.4 2.1 fusion.113
  367.2 5.1 collective-permute-done.12
  376.7 1.8 select_select_fusion.1
  378.5 17.0 %all-gather.22.cloned.1.call-done = bf16[2048,1024]{1,0:T(8,128)(2,1)} async-done(((bf16[128,1024]{1,0:T(8,128)(2,1)}), bf16[2048,1024]{1,0:T(8,128)(2,1)}) %all-gather.22.cloned.1.call-update) | async-done | bytes 4194320 | tf_op jit(solution)/shard_map/all_gather | solution.py:432
  395.5 4.8 convolution_add_fusion.2
  400.2 46.6 %all-gather.16.cloned.1.call-done = bf16[16,128,1024]{2,1,0:T(8,128)(2,1)} async-done(((bf16[1,128,1024]{2,1,0:T(8,128)(2,1)}), bf16[16,128,1024]{2,1,0:T(8,128)(2,1)}) %all-gather.16.cloned.1.call-update) | async-done | bytes 4194320 | tf_op jit(solution)/shard_map/all_gather | solution.py:432
  446.8 8.6 %fusion.18 = f32[1024,256]{1,0:T(8,128)S(1)} fusion(bf16[2048,1024]{1,0:T(8,128)(2,1)} %all-gather.22.cloned.1.call-done, bf16[2048,1024]{1,0:T(8,128)(2,1)} %bitcast.222, f32[2048,256]{1,0:T(8,128)} %convolution_add_fusion.2, bf16[128,1024]{1,0:T(8,128)(2,1)S(1)} %get-tuple-element.88, bf16[128,1024]{1,0:T(8,128)(2,1)S(1)} %get-tuple-element.87), kind=kOutput, calls=%fused_computation.51 | convolution fusion | flops 2153775104 | bytes 12058624 | tf_op jit(solution)/shard_map/dot_general | solution.py:21
  455.4 1.5 collective-permute-start.13
  457.0 7.0 %collective-permute-done.13 = bf16[512,256]{1,0:T(8,128)(2,1)S(1)} collective-permute-done((bf16[512,256]{1,0:T(8,128)(2,1)S(1)}, bf16[512,256]{1,0:T(8,128)(2,1)S(1)}, u32[]{:S(2)}, u32[]{:S(2)}) %collective-permute-start.13) | collective-permute-done | bytes 262176 | tf_op jit(solution)/shard_map/ppermute | solution.py:394
  464.8 4.1 fusion.17
  469.0 1.5 collective-permute-start.14
  470.5 6.3 collective-permute-done.14
  477.6 2.7 constant_dynamic-slice_fusion.13
  480.3 1.5 collective-permute-start.10
  483.3 3.6 all-to-all-start.2
  487.0 28.7 %collective-permute-done.10 = bf16[256,3072]{1,0:T(8,128)(2,1)} collective-permute-done((bf16[256,3072]{1,0:T(8,128)(2,1)}, bf16[256,3072]{1,0:T(8,128)(2,1)}, u32[]{:S(2)}, u32[]{:S(2)}) %collective-permute-start.10) | collective-permute-done | bytes 1572896 | tf_op jit(solution)/shard_map/ppermute | solution.py:394
  515.7 3.5 fusion.42
  519.3 2.2 convolution_add_fusion.4
  522.8 3.1 convolution_dynamic-update-slice_fusion.3
  525.9 2.1 convolution_dynamic-update-slice_fusion.6
  528.0 2.2 convolution_dynamic-update-slice_fusion.5
  531.8 59.8 %psum.7 = f32[1,11264]{1,0:T(1,128)S(1)} all-reduce(f32[1,11264]{1,0:T(1,128)S(1)} %bitcast.204), channel_id=1, replica_groups=mesh['ctx'=16,'fsdp'=2] {'ctx'}, use_global_device_ids=true, to_apply=%region_15.16 | all-reduce | flops 11264 | bytes 90112 | tf_op jit(solution)/shard_map/psum | solution.py:562
  591.6 4.7 all-gather.5
  601.5 2.8 convert_element_type.324
  604.3 5.4 copy.45
  609.8 6.6 copy.47
  616.4 9.2 %reshape.402 = f32[16,512,2,128]{3,2,1,0:T(2,128)} reshape(bf16[8192,256]{1,0:T(8,128)(2,1)} %all-gather.24.cloned.1.call-done) | data formatting | bytes 12582912 | tf_op jit(solution)/shard_map/convert_element_type | solution.py:629
  625.5 8.3 %copy.46 = f32[512,2,16,128]{3,2,1,0:T(8,128)S(1)} copy(f32[512,2,16,128]{3,1,0,2:T(2,128)} %bitcast.186) | data formatting | bytes 16777216 | tf_op jit(solution)/shard_map/convert_element_type | solution.py:629
  633.8 11.7 %copy.61 = f32[64,8,32,128]{3,1,2,0:T(8,128)} copy(f32[64,8,32,128]{3,2,1,0:T(8,128)S(1)} %bitcast.187) | data formatting | bytes 16777216
  645.5 6.7 %convert_element_type.325 = f32[2048,1024]{1,0:T(8,128)} convert(bf16[2048,1024]{1,0:T(8,128)(2,1)} %all-gather.26.cloned.1.call-done) | non-fusion elementwise | flops 2097152 | bytes 12582912 | tf_op jit(solution)/shard_map/convert_element_type | solution.py:623
  (198 shorter events, 42.7 us)
Async XLA Ops:
  7.2 16.0 %copy-start = (bf16[512,1024]{1,0:T(8,128)(2,1)S(1)}, bf16[512,1024]{1,0:T(8,128)(2,1)}, u32[]{:S(2)}) copy-start(bf16[512,1024]{1,0:T(8,128)(2,1)} %param.17) | copy-start | bytes 3145732
  7.2 17.5 %copy-start.26 = (u32[32]{0:T(128)S(1)}, u32[32]{0:T(128)}, u32[]{:S(2)}) copy-start(u32[32]{0:T(128)} %constant.177) | copy-start | bytes 388
  7.2 139.2 %all-gather.14.cloned.1.call-start = ((), (), s32[]{:S(2)}) async-start(), calls=%async_computation.4 | async-start | bytes 4456448 | tf_op jit(solution)/shard_map/all_gather | solution.py:432
  9.6 94.7 %collective-permute-start.1 = (bf16[64,2048]{1,0:T(8,128)(2,1)}, bf16[64,2048]{1,0:T(8,128)(2,1)}, u32[]{:S(2)}, u32[]{:S(2)}) collective-permute-start(bf16[64,2048]{1,0:T(8,128)(2,1)} %constant_dynamic-slice_fusion.21), channel_id=1, source_target_pairs={{0,1},{1,0},{2,3},{3,2},{4,5},{5,4},{6,7},{7,6},{8,9},{9,8},{10,11... | collective-permute-start | bytes 786440 | tf_op jit(solution)/shard_map/ppermute | solution.py:394
  18.3 81.5 %collective-permute-start = (bf16[1,4608]{1,0:T(2,128)(2,1)}, bf16[1,4608]{1,0:T(2,128)(2,1)}, u32[]{:S(2)}, u32[]{:S(2)}) collective-permute-start(bf16[1,4608]{1,0:T(2,128)(2,1)} %broadcast_in_dim.87), channel_id=1, source_target_pairs={{0,1},{1,0},{2,3},{3,2},{4,5},{5,4},{6,7},{7,6},{8,9},{9,8},{10,11... | collective-permute-start | bytes 27656 | tf_op jit(solution)/shard_map/ppermute | solution.py:394
  18.4 2.7 copy-start.25
  19.6 0.7 copy-start.12
  19.6 1.5 copy-start.13
  21.2 83.7 %collective-permute-start.3 = (bf16[512,256]{1,0:T(8,128)(2,1)}, bf16[512,256]{1,0:T(8,128)(2,1)}, u32[]{:S(2)}, u32[]{:S(2)}) collective-permute-start(bf16[512,256]{1,0:T(8,128)(2,1)} %maximum_maximum_fusion), channel_id=1, source_target_pairs={{0,1},{1,0},{2,3},{3,2},{4,5},{5,4},{6,7},{7,6},{8,9},{9,8},{10,11... | collective-permute-start | bytes 786440 | tf_op jit(solution)/shard_map/ppermute | solution.py:394
  24.0 84.1 %collective-permute-start.4 = (bf16[256,1024]{1,0:T(8,128)(2,1)}, bf16[256,1024]{1,0:T(8,128)(2,1)}, u32[]{:S(2)}, u32[]{:S(2)}) collective-permute-start(bf16[256,1024]{1,0:T(8,128)(2,1)} %constant_dynamic-slice_fusion.16), channel_id=1, source_target_pairs={{0,1},{1,0},{2,3},{3,2},{4,5},{5,4},{6,7},{7,6},{8,9},{9,8},{10,11... | collective-permute-start | bytes 1572872 | tf_op jit(solution)/shard_map/ppermute | solution.py:394
  27.8 75.2 %collective-permute-start.8 = (bf16[1024,1024]{1,0:T(8,128)(2,1)S(1)}, bf16[1024,1024]{1,0:T(8,128)(2,1)}, u32[]{:S(2)}, u32[]{:S(2)}) collective-permute-start(bf16[1024,1024]{1,0:T(8,128)(2,1)S(1)} %constant_dynamic-slice_fusion.14), channel_id=1, source_target_pairs={{0,1},{1,0},{2,3},{3,2},{4,5},{5,4},{6,7},{7,6},{8,9},{9,8},{10,11... | collective-permute-start | bytes 6291464 | tf_op jit(solution)/shard_map/ppermute | solution.py:394
  86.3 3.7 copy-start.21
  86.3 3.7 copy-start.23
  93.1 1.5 copy-start.6
  99.9 9.3 %copy-start.18 = (f32[1,2048]{1,0:T(1,128)S(1)}, f32[1,2048]{1,0:T(1,128)}, u32[]{:S(2)}) copy-start(f32[1,2048]{1,0:T(1,128)} %fusion.74) | copy-start | bytes 24580
  99.9 46.5 %collective-permute-start.6 = (bf16[256,4096]{1,0:T(8,128)(2,1)}, bf16[256,4096]{1,0:T(8,128)(2,1)}, u32[]{:S(2)}, u32[]{:S(2)}) collective-permute-start(bf16[256,4096]{1,0:T(8,128)(2,1)} %constant_dynamic-slice_fusion.15), channel_id=1, source_target_pairs={{0,1},{1,0},{2,3},{3,2},{4,5},{5,4},{6,7},{7,6},{8,9},{9,8},{10,11... | collective-permute-start | bytes 6291464 | tf_op jit(solution)/shard_map/ppermute | solution.py:394
  103.0 75.6 %collective-permute-start.9 = (bf16[1024,1024]{1,0:T(8,128)(2,1)}, bf16[1024,1024]{1,0:T(8,128)(2,1)S(1)}, u32[]{:S(2)}, u32[]{:S(2)}) collective-permute-start(bf16[1024,1024]{1,0:T(8,128)(2,1)} %collective-permute-done.8), channel_id=1, source_target_pairs={{0,2},{2,0},{4,6},{6,4},{8,10},{10,8},{12,14},{14,12},{16,18},{18,... | collective-permute-start | bytes 6291464 | tf_op jit(solution)/shard_map/ppermute | solution.py:397
  104.3 3.9 collective-permute-start.2
  108.2 79.6 %collective-permute-start.5 = (bf16[256,1024]{1,0:T(8,128)(2,1)}, bf16[256,1024]{1,0:T(8,128)(2,1)}, u32[]{:S(2)}, u32[]{:S(2)}) collective-permute-start(bf16[256,1024]{1,0:T(8,128)(2,1)} %collective-permute-done.4), channel_id=1, source_target_pairs={{0,2},{2,0},{4,6},{6,4},{8,10},{10,8},{12,14},{14,12},{16,18},{18,... | collective-permute-start | bytes 1572872 | tf_op jit(solution)/shard_map/ppermute | solution.py:397
  146.4 48.4 %collective-permute-start.7 = (bf16[256,4096]{1,0:T(8,128)(2,1)}, bf16[256,4096]{1,0:T(8,128)(2,1)}, u32[]{:S(2)}, u32[]{:S(2)}) collective-permute-start(bf16[256,4096]{1,0:T(8,128)(2,1)} %collective-permute-done.6), channel_id=1, source_target_pairs={{0,2},{2,0},{4,6},{6,4},{8,10},{10,8},{12,14},{14,12},{16,18},{18,... | collective-permute-start | bytes 6291464 | tf_op jit(solution)/shard_map/ppermute | solution.py:397
  169.0 16.1 %all-to-all-start = ((bf16[16,64,128]{2,1,0:T(8,128)(2,1)}), bf16[16,64,128]{2,1,0:T(8,128)(2,1)}, u32[]{:S(2)}, u32[]{:S(2)}) async-start(bf16[16,64,128]{2,1,0:T(8,128)(2,1)} %get-tuple-element.25), calls=%async_computation | async-start | bytes 524288 | tf_op jit(solution)/shard_map/all_to_all | solution.py:495
  175.1 170.7 %reduce-scatter.2.cloned.1.call-start = ((), (), s32[]{:S(2)}) async-start(), calls=%async_computation.5 | async-start | bytes 2162688 | tf_op jit(solution)/shard_map/reduce_scatter | solution.py:632
  178.6 7.8 %copy-start.3 = (bf16[1024,1024]{1,0:T(8,128)(2,1)}, bf16[1024,1024]{1,0:T(8,128)(2,1)S(1)}, u32[]{:S(2)}) copy-start(bf16[1024,1024]{1,0:T(8,128)(2,1)S(1)} %collective-permute-done.9) | copy-start | bytes 6291460
  180.2 7.6 %copy-start.5 = (bf16[1,128,1024]{2,1,0:T(8,128)(2,1)S(1)}, bf16[1,128,1024]{2,1,0:T(8,128)(2,1)}, u32[]{:S(2)}) copy-start(bf16[1,128,1024]{2,1,0:T(8,128)(2,1)} %param.15) | copy-start | bytes 786436
  189.6 5.2 copy-start.11
  192.6 2.1 copy-start.20
  194.8 4.8 copy-start.2
  203.6 2.8 copy-start.7
  210.5 185.0 %all-gather.22.cloned.1.call-start = ((), (), s32[]{:S(2)}) async-start(), calls=%async_computation.9 | async-start | bytes 4456448 | tf_op jit(solution)/shard_map/all_gather | solution.py:432
  211.2 235.6 %all-gather.16.cloned.1.call-start = ((), (), s32[]{:S(2)}) async-start(), calls=%async_computation.6 | async-start | bytes 4456448 | tf_op jit(solution)/shard_map/all_gather | solution.py:432
  218.1 127.8 %all-to-all-start.1 = ((bf16[16,64,128]{2,1,0:T(8,128)(2,1)}), bf16[16,64,128]{2,1,0:T(8,128)(2,1)S(1)}, u32[]{:S(2)}, u32[]{:S(2)}) async-start(bf16[16,64,128]{2,1,0:T(8,128)(2,1)} %bitcast.22), calls=%async_computation.1 | async-start | bytes 524288 | tf_op jit(solution)/shard_map/all_to_all | solution.py:522
  221.6 379.9 %all-gather.20.cloned.1.call-start = ((), (), s32[]{:S(2)}) async-start(), calls=%async_computation.8 | async-start | bytes 1114112 | tf_op jit(solution)/shard_map/all_gather | solution.py:432
  345.8 258.5 %all-gather.18.cloned.1.call-start = ((), (), s32[]{:S(2)}) async-start(), calls=%async_computation.7 | async-start | bytes 3342336 | tf_op jit(solution)/shard_map/all_gather | solution.py:432
  345.9 0.7 copy-start.15
  346.6 17.8 %copy-start.8 = (bf16[2048,1024]{1,0:T(8,128)(2,1)S(1)}, bf16[2048,1024]{1,0:T(8,128)(2,1)}, u32[]{:S(2)}) copy-start(bf16[2048,1024]{1,0:T(8,128)(2,1)} %get-tuple-element.30) | copy-start | bytes 12582916
  366.5 8.2 %copy-start.17 = (f32[1,1,2,2048]{3,2,1,0:T(2,128)S(1)}, f32[1,1,2,2048]{3,2,1,0:T(2,128)}, u32[]{:S(2)}) copy-start(f32[1,1,2,2048]{3,2,1,0:T(2,128)} %get-tuple-element.83) | copy-start | bytes 49156
  366.6 5.7 collective-permute-start.12
  373.1 243.3 %all-gather.24.cloned.1.call-start = ((), (), s32[]{:S(2)}) async-start(), calls=%async_computation.10 | async-start | bytes 4456448 | tf_op jit(solution)/shard_map/all_gather | solution.py:432
  455.4 8.5 %collective-permute-start.13 = (bf16[512,256]{1,0:T(8,128)(2,1)S(1)}, bf16[512,256]{1,0:T(8,128)(2,1)S(1)}, u32[]{:S(2)}, u32[]{:S(2)}) collective-permute-start(bf16[512,256]{1,0:T(8,128)(2,1)S(1)} %dynamic-slice_convert_fusion.1), channel_id=1, source_target_pairs={{0,1},{1,0},{2,3},{3,2},{4,5},{5,4},{6,7},{7,6},{8,9},{9,8},{10,11... | collective-permute-start | bytes 786440 | tf_op jit(solution)/shard_map/ppermute | solution.py:394
  464.8 180.8 %all-gather.26.cloned.1.call-start = ((), (), s32[]{:S(2)}) async-start(), calls=%async_computation.11 | async-start | bytes 4456448 | tf_op jit(solution)/shard_map/all_gather | solution.py:432
  469.0 12.8 %copy-start.22 = (bf16[2,1,128]{2,0,1:T(2,128)(2,1)S(1)}, bf16[2,1,128]{2,0,1:T(2,128)(2,1)}, u32[]{:S(2)}) copy-start(bf16[2,1,128]{2,0,1:T(2,128)(2,1)} %copy-done.21) | copy-start | bytes 1540
  469.0 12.8 %copy-start.24 = (bf16[2,1,128]{2,0,1:T(2,128)(2,1)S(1)}, bf16[2,1,128]{2,0,1:T(2,128)(2,1)}, u32[]{:S(2)}) copy-start(bf16[2,1,128]{2,0,1:T(2,128)(2,1)} %copy-done.23) | copy-start | bytes 1540
  469.0 7.8 %collective-permute-start.14 = (bf16[128,1024]{1,0:T(8,128)(2,1)S(1)}, bf16[128,1024]{1,0:T(8,128)(2,1)S(1)}, u32[]{:S(2)}, u32[]{:S(2)}) collective-permute-start(bf16[128,1024]{1,0:T(8,128)(2,1)S(1)} %dynamic-slice_convert_fusion), channel_id=1, source_target_pairs={{0,1},{1,0},{2,3},{3,2},{4,5},{5,4},{6,7},{7,6},{8,9},{9,8},{10,11... | collective-permute-start | bytes 786440 | tf_op jit(solution)/shard_map/ppermute | solution.py:394
  477.6 4.6 copy-start.19
  477.6 4.6 copy-start.9
  480.3 6.6 %copy-start.16 = (f32[2,1024]{1,0:T(2,128)S(1)}, f32[2,1024]{1,0:T(2,128)}, u32[]{:S(2)}) copy-start(f32[2,1024]{1,0:T(2,128)} %get-tuple-element.122.gains_ref) | copy-start | bytes 24580
  480.3 35.4 %collective-permute-start.10 = (bf16[256,3072]{1,0:T(8,128)(2,1)}, bf16[256,3072]{1,0:T(8,128)(2,1)}, u32[]{:S(2)}, u32[]{:S(2)}) collective-permute-start(bf16[256,3072]{1,0:T(8,128)(2,1)} %constant_dynamic-slice_fusion.13), channel_id=1, source_target_pairs={{0,1},{1,0},{2,3},{3,2},{4,5},{5,4},{6,7},{7,6},{8,9},{9,8},{10,11... | collective-permute-start | bytes 4718600 | tf_op jit(solution)/shard_map/ppermute | solution.py:394
  483.3 39.4 %all-to-all-start.2 = ((bf16[16,192,128]{2,1,0:T(8,128)(2,1)}), bf16[16,192,128]{2,1,0:T(8,128)(2,1)S(1)}, u32[]{:S(2)}, u32[]{:S(2)}) async-start(bf16[16,192,128]{2,1,0:T(8,128)(2,1)} %bitcast_bitcast_fusion), calls=%async_computation.2 | async-start | bytes 1572864 | tf_op jit(solution)/shard_map/all_to_all | solution.py:532
  515.7 12.3 %collective-permute-start.11 = (bf16[256,3072]{1,0:T(8,128)(2,1)}, bf16[256,3072]{1,0:T(8,128)(2,1)}, u32[]{:S(2)}, u32[]{:S(2)}) collective-permute-start(bf16[256,3072]{1,0:T(8,128)(2,1)} %collective-permute-done.10), channel_id=1, source_target_pairs={{0,2},{2,0},{4,6},{6,4},{8,10},{10,8},{12,14},{14,12},{16,18},{18,... | collective-permute-start | bytes 4718600 | tf_op jit(solution)/shard_map/ppermute | solution.py:397
  515.7 3.6 copy-start.14
  519.3 2.2 copy-start.4
  528.0 2.6 copy-start.10
  645.5 6.7 %copy-start.1 = (bf16[512,1024]{1,0:T(8,128)(2,1)S(1)}, bf16[512,1024]{1,0:T(8,128)(2,1)}, u32[]{:S(2)}) copy-start(bf16[512,1024]{1,0:T(8,128)(2,1)} %param.17) | copy-start | bytes 3145732
Sparse Core Ops, SparseCore 0:
  10.2 53.2 all-gather.13
  210.6 135.1 reduce-scatter.1
  348.2 47.2 all-gather.21
  397.7 49.0 all-gather.15
  449.0 36.4 all-gather.19
  487.9 48.6 all-gather.17
  538.9 49.7 all-gather.23
  591.1 49.1 all-gather.25

commit v2 on v1

--- a/solution.py
+++ b/solution.py
@@ -3,6 +3,7 @@
 
 import jax
 import jax.numpy as jnp
+import numpy as np
 from jax import lax
 from jax.experimental import pallas as pl
 from jax.experimental.pallas import tpu as pltpu
@@ -124,7 +125,10 @@
     pair_ref[...] = jnp.concatenate([value, query], axis=0).T.astype(BF16)
 
 
-def attend_kernel(chunk, rows, query_ref, key_ref, value_ref, out_ref, sent_ref, lse_ref, score_ref):
+def attend_kernel(
+    chunk, rows, place_ref, query_ref, key_ref, value_ref, out_ref, sent_ref, lse_ref, score_ref,
+):
+    core = place_ref[0] % 2
     count = key_ref.shape[0]
     query = query_ref[...]
     top = None
@@ -146,15 +150,17 @@
     out = out / total
     out_ref[...] = out
     for at in range(sent_ref.shape[0]):
-        sent_ref[at] = out[:, at * rows : (at + 1) * rows].astype(BF16)
+        sent_ref[at ^ core] = out[:, at * rows : (at + 1) * rows].astype(BF16)
     lse_ref[...] = top + jnp.log(total)
 
 
 def attend_back_kernel(
-    chunk, rows, head_size, query_ref, grad_ref, out_ref, lse_ref, key_ref, key_t_ref, pair_ref,
-    pair_block_ref, cos_block_ref, sin_block_ref, cos_ref, sin_ref, mixed_ref, key_acc, value_acc,
+    chunk, rows, head_size, place_ref, query_ref, grad_ref, out_ref, lse_ref, key_ref, key_t_ref, pair_ref,
+    pair_block_ref, cos_block_ref, sin_block_ref, cos_ref, sin_ref, mixed_ref, sent_ref, key_acc, value_acc,
 ):
     step = pl.program_id(0)
+    core = place_ref[0] % 2
+    per_step = grad_ref.shape[0]
     count = key_ref.shape[0]
     block = query_ref.shape[1]
     half = head_size // 2
@@ -167,7 +173,7 @@
 
     query = query_ref[...]
     grad = jnp.concatenate(
-        [grad_ref[at] for at in range(grad_ref.shape[0])], axis=1
+        [grad_ref[at ^ core] for at in range(per_step)], axis=1
     ).astype(F32)
     delta = jnp.sum(grad * out_ref[...], axis=0, keepdims=True)
     lse = lse_ref[...]
@@ -200,18 +206,27 @@
         ).astype(BF16)
 
     at = pl.multiple_of(step * block, block)
-    mixed_ref[0:head_size, pl.ds(at, block)] = turn_back(
+    query_part = turn_back(
         grad_query * scale, cos_block_ref[...], sin_block_ref[...]
     )
+    mixed_ref[0:head_size, pl.ds(at, block)] = query_part
+    for k in range(per_step):
+        sent_ref[place_ref[step * per_step + k], 0:head_size, :] = query_part[
+            :, k * rows : (k + 1) * rows
+        ]
 
     @pl.when(step == pl.num_programs(0) - 1)
     def _():
-        mixed_ref[head_size : 2 * head_size, :] = turn_back(
+        key_part = turn_back(
             key_acc[...].T[head_size : 2 * head_size], cos_ref[...], sin_ref[...]
         )
-        mixed_ref[2 * head_size : 3 * head_size, :] = value_acc[...].T[
-            :head_size
-        ].astype(BF16)
+        value_part = value_acc[...].T[:head_size].astype(BF16)
+        both = jnp.concatenate([key_part, value_part], axis=0)
+        mixed_ref[head_size : 3 * head_size, :] = both
+        for k in range(count // rows):
+            sent_ref[place_ref[k], head_size : 3 * head_size, :] = both[
+                :, k * rows : (k + 1) * rows
+            ]
 
 
 def whole(shape):
@@ -262,30 +277,36 @@
     )(ends, base, tokens, gains, shifts, w_head, cos, sin)
 
 
-def attend(query_t, key, value_t, rows):
+def attend(place, query_t, key, value_t, rows):
     count = key.shape[0]
     head_size = value_t.shape[0]
     block = min(count, 2 * rows)
     chunk = min(count, 512)
+    grid_spec = pltpu.PrefetchScalarGridSpec(
+        num_scalar_prefetch=1,
+        grid=(count // block,),
+        in_specs=[
+            pl.BlockSpec((128, block), lambda i, _: (0, i)),
+            whole((count, 128)),
+            whole((head_size, count)),
+        ],
+        out_specs=[
+            pl.BlockSpec((head_size, block), lambda i, _: (0, i)),
+            pl.BlockSpec(
+                (2, head_size, rows), lambda i, place: (place[2 * i] // 2, 0, 0)
+            ),
+            pl.BlockSpec((1, block), lambda i, _: (0, i)),
+        ],
+        scratch_shapes=[pltpu.VMEM((count, block), F32)],
+    )
     return pl.pallas_call(
         functools.partial(attend_kernel, chunk, rows),
-        grid=(count // block,),
-        in_specs=[
-            pl.BlockSpec((128, block), lambda i: (0, i)),
-            whole((count, 128)),
-            whole((head_size, count)),
-        ],
-        out_specs=[
-            pl.BlockSpec((head_size, block), lambda i: (0, i)),
-            pl.BlockSpec((block // rows, head_size, rows), lambda i: (i, 0, 0)),
-            pl.BlockSpec((1, block), lambda i: (0, i)),
-        ],
+        grid_spec=grid_spec,
         out_shape=[
             jax.ShapeDtypeStruct((head_size, count), F32),
             jax.ShapeDtypeStruct((count // rows, head_size, rows), BF16),
             jax.ShapeDtypeStruct((1, count), F32),
         ],
-        scratch_shapes=[pltpu.VMEM((count, block), F32)],
         compiler_params=pltpu.CompilerParams(vmem_limit_bytes=VMEM_BYTES),
         cost_estimate=pl.CostEstimate(
             flops=8 * count * count * 128,
@@ -293,35 +314,47 @@
             transcendentals=count * count,
         ),
         name="attend_head",
-    )(query_t, key, value_t)
-
-
-def attend_back(query_t, grad, out, lse, key, key_t, pair, cos, sin, rows):
+    )(place, query_t, key, value_t)
+
+
+def attend_back(place, query_t, grad, out, lse, key, key_t, pair, cos, sin, rows):
     count = key.shape[0]
     head_size = key_t.shape[0]
     half = head_size // 2
     block = min(count, 2 * rows)
     chunk = min(count, 512)
-    return pl.pallas_call(
-        functools.partial(attend_back_kernel, chunk, rows, head_size),
+    grid_spec = pltpu.PrefetchScalarGridSpec(
+        num_scalar_prefetch=1,
         grid=(count // block,),
         in_specs=[
-            pl.BlockSpec((128, block), lambda i: (0, i)),
-            pl.BlockSpec((block // rows, head_size, rows), lambda i: (i, 0, 0)),
-            pl.BlockSpec((head_size, block), lambda i: (0, i)),
-            pl.BlockSpec((1, block), lambda i: (0, i)),
+            pl.BlockSpec((128, block), lambda i, _: (0, i)),
+            pl.BlockSpec(
+                (2, head_size, rows), lambda i, place: (place[2 * i] // 2, 0, 0)
+            ),
+            pl.BlockSpec((head_size, block), lambda i, _: (0, i)),
+            pl.BlockSpec((1, block), lambda i, _: (0, i)),
             whole((count, 128)),
             whole((head_size, count)),
             whole((count, 128)),
-            pl.BlockSpec((block, 128), lambda i: (i, 0)),
-            pl.BlockSpec((half, block), lambda i: (0, i)),
-            pl.BlockSpec((half, block), lambda i: (0, i)),
+            pl.BlockSpec((block, 128), lambda i, _: (i, 0)),
+            pl.BlockSpec((half, block), lambda i, _: (0, i)),
+            pl.BlockSpec((half, block), lambda i, _: (0, i)),
             whole((half, count)),
             whole((half, count)),
         ],
-        out_specs=whole((3 * head_size, count)),
-        out_shape=jax.ShapeDtypeStruct((3 * head_size, count), BF16),
+        out_specs=[
+            whole((3 * head_size, count)),
+            whole((count // rows, 3 * head_size, rows)),
+        ],
         scratch_shapes=[pltpu.VMEM((count, 128), F32), pltpu.VMEM((count, 128), F32)],
+    )
+    return pl.pallas_call(
+        functools.partial(attend_back_kernel, chunk, rows, head_size),
+        grid_spec=grid_spec,
+        out_shape=[
+            jax.ShapeDtypeStruct((3 * head_size, count), BF16),
+            jax.ShapeDtypeStruct((count // rows, 3 * head_size, rows), BF16),
+        ],
         compiler_params=pltpu.CompilerParams(vmem_limit_bytes=VMEM_BYTES),
         cost_estimate=pl.CostEstimate(
             flops=20 * count * count * 128,
@@ -329,47 +362,185 @@
             transcendentals=count * count,
         ),
         name="attend_head_back",
-    )(query_t, grad, out, lse, key, key_t, pair, pair, cos, sin, cos, sin)
-
-
-def times_rows(values, pieces):
-    return sum(
-        jnp.dot(
-            lax.dynamic_slice_in_dim(values, at, piece.shape[0], 1),
-            piece,
+    )(place, query_t, grad, out, lse, key, key_t, pair, pair, cos, sin, cos, sin)
+
+
+def up_kernel(in_ref, out_ref):
+    for j in range(in_ref.shape[0]):
+        out_ref[:, j * 128 : (j + 1) * 128] = in_ref[j].astype(F32)
+
+
+def down_kernel(in_ref, out_ref):
+    for j in range(in_ref.shape[0]):
+        for k in range(out_ref.shape[1] // 128):
+            out_ref[j * 128 : (j + 1) * 128, k * 128 : (k + 1) * 128] = in_ref[
+                j, k * 128 : (k + 1) * 128, :
+            ].astype(F32)
+
+
+def expand_up(packed, up_rows, shards):
+    devices = packed.shape[0]
+    many = min(devices, 8)
+    groups = devices // many
+    return pl.pallas_call(
+        up_kernel,
+        grid=(shards, groups),
+        in_specs=[pl.BlockSpec((many, up_rows, 128), lambda k, g: (g, k, 0))],
+        out_specs=pl.BlockSpec((up_rows, many * 128), lambda k, g: (0, k * groups + g)),
+        out_shape=jax.ShapeDtypeStruct((up_rows, shards * devices * 128), F32),
+        compiler_params=pltpu.CompilerParams(vmem_limit_bytes=VMEM_BYTES),
+        name="expand_up",
+    )(packed)
+
+
+def expand_down(packed, width):
+    devices = packed.shape[0]
+    many = 4
+    return pl.pallas_call(
+        down_kernel,
+        grid=(devices // many,),
+        in_specs=[pl.BlockSpec((many, width, 128), lambda g: (g, 1, 0))],
+        out_specs=pl.BlockSpec((many * 128, width), lambda g: (g, 0)),
+        out_shape=jax.ShapeDtypeStruct((devices * 128, width), F32),
+        compiler_params=pltpu.CompilerParams(vmem_limit_bytes=VMEM_BYTES),
+        name="expand_down",
+    )(packed)
+
+
+def last_kernel(head_size, place_ref, where_ref, in_ref, qkv_ref, out_ref):
+    chip = pl.program_id(0)
+    core = place_ref[0] % 2
+    width = out_ref.shape[1]
+    depth = in_ref.shape[2]
+    pair = [in_ref[at ^ core] for at in range(2)]
+    for k in range(3):
+        part = slice(k * head_size, (k + 1) * head_size)
+        both = jnp.concatenate([pair[0][part], pair[1][part]], axis=0).astype(F32)
+        at = pl.multiple_of(k * width + chip * 2 * head_size, 128)
+        qkv_ref[:, pl.ds(at, 2 * head_size)] = both.T
+    rows = out_ref.shape[0] // 2
+    top = 3 * head_size
+    for at in range(2):
+        for k in range(width // depth):
+            out_ref[at * rows : (at + 1) * rows, k * depth : (k + 1) * depth] = pair[at][
+                top + k * rows : top + (k + 1) * rows
+            ].astype(F32)
+
+
+def expand_last(place, where, packed, width, head_size):
+    devices, tall, depth = packed.shape
+    grid_spec = pltpu.PrefetchScalarGridSpec(
+        num_scalar_prefetch=2,
+        grid=(devices // 2,),
+        in_specs=[
+            pl.BlockSpec((2, tall, depth), lambda i, place, where: (where[i], 0, 0))
+        ],
+        out_specs=[
+            whole((depth, 3 * width)),
+            pl.BlockSpec((2 * (depth // devices), width), lambda i, *_: (i, 0)),
+        ],
+    )
+    return pl.pallas_call(
+        functools.partial(last_kernel, head_size),
+        grid_spec=grid_spec,
+        out_shape=[
+            jax.ShapeDtypeStruct((depth, 3 * width), F32),
+            jax.ShapeDtypeStruct((depth, width), F32),
+        ],
+        compiler_params=pltpu.CompilerParams(vmem_limit_bytes=VMEM_BYTES),
+        name="expand_last",
+    )(place, where, packed)
+
+
+def times(values, blocks, columns):
+    total = None
+    placed = {}
+    for block, row, column in blocks:
+        term = jnp.dot(
+            lax.dynamic_slice_in_dim(values, row, block.shape[0], 1),
+            block,
             preferred_element_type=F32,
         )
-        for piece, at in pieces
-    )
-
-
-def times_rows_t(values_t, pieces):
-    return sum(
-        dims(lax.dynamic_slice_in_dim(values_t, at, piece.shape[0], 0), piece, 0, 0)
-        for piece, at in pieces
-    )
-
-
-def joined(parts, pieces, dim):
-    if len(parts) == 1:
-        return parts[0]
-    shape = list(parts[0].shape)
-    shape[dim] = sum(part.shape[dim] for part in parts)
-    out = jnp.zeros(shape, parts[0].dtype)
-    for part, (_, at) in zip(parts, pieces):
-        out = lax.dynamic_update_slice_in_dim(out, part, at, dim)
+        if block.shape[1] == columns:
+            total = term if total is None else total + term
+        elif id(column) in placed:
+            placed[id(column)][0] += term
+        else:
+            placed[id(column)] = [term, column]
+    if placed:
+        side = jnp.zeros(total.shape, F32)
+        for term, column in placed.values():
+            side = lax.dynamic_update_slice_in_dim(side, term, column, 1)
+        total = total + side
+    return total
+
+
+def times_t(values, blocks, length):
+    found = {}
+    for block, row, column in blocks:
+        part = values
+        if block.shape[1] != values.shape[1]:
+            part = lax.dynamic_slice_in_dim(values, column, block.shape[1], 1)
+        term = dims(part, block, 1, 1)
+        if id(row) in found:
+            found[id(row)][0] += term
+        else:
+            found[id(row)] = [term, row]
+    if len(found) == 1:
+        return term
+    out = jnp.zeros((values.shape[0], length), F32)
+    for term, row in found.values():
+        out = lax.dynamic_update_slice_in_dim(out, term, row, 1)
     return out
 
 
-def rows_of(pieces, start, size):
-    out = None
-    for piece, at in pieces:
-        length = piece.shape[0]
-        local = jnp.clip(start - at, 0, length - size)
-        found = lax.dynamic_slice_in_dim(piece, local, size, 0)
-        inside = (start >= at) & (start < at + length)
-        out = found if out is None else jnp.where(inside, found, out)
+def columns_of(blocks, start, size, length):
+    found = {}
+    for block, row, column in blocks:
+        last = block.shape[1] - size
+        local = jnp.clip(start - column, 0, last)
+        part = lax.dynamic_slice_in_dim(block, local, size, 1)
+        if id(row) in found:
+            inside = (start >= column) & (start <= column + last)
+            found[id(row)][0] = jnp.where(inside, part, found[id(row)][0])
+        else:
+            found[id(row)] = [part, row]
+    if len(found) == 1:
+        return part
+    out = jnp.zeros((length, size), blocks[0][0].dtype)
+    for part, row in found.values():
+        out = lax.dynamic_update_slice_in_dim(out, part, row, 0)
     return out
+
+
+def ring_chips(chips):
+    if chips == 8:
+        return [0, 2, 4, 6, 7, 5, 3, 1]
+    return list(range(chips))
+
+
+def ring_tables(ctx_size):
+    chips = ctx_size // 2
+    order = ring_chips(chips)
+    offsets = [0]
+    for step in range(1, chips // 2 + 1):
+        offsets.append(-step)
+        if step <= (chips - 1) // 2:
+            offsets.append(step)
+    place = np.zeros((ctx_size, ctx_size), np.int32)
+    where = np.zeros((ctx_size, chips), np.int32)
+    for me in range(ctx_size):
+        at = order.index(me // 2)
+        for k, offset in enumerate(offsets):
+            chip = order[(at + offset) % chips]
+            place[me, 2 * k] = 2 * chip + me % 2
+            place[me, 2 * k + 1] = 2 * chip + 1 - me % 2
+            where[me, chip] = k
+    return order, place, where
+
+
+def after(values, *earlier):
+    return lax.optimization_barrier((values, *earlier))[0]
 
 
 def body(
@@ -389,34 +560,85 @@
     seq_count = lengths.shape[1]
     hidden = w_up.shape[1]
     paired = fsdp_size == 2
+    other = 1 - shard
+    chips = ctx_size // 2
+    order, place_table, where_table = ring_tables(ctx_size)
+    place = jnp.asarray(place_table)[me]
+    where = jnp.asarray(where_table)[me]
 
     def across(values):
         return lax.ppermute(values, "fsdp", [(0, 1), (1, 0)])
 
-    def core_swap(values):
-        return lax.ppermute(values, "ctx", [(i, i ^ 1) for i in range(ctx_size)])
-
-    def gather_small(values):
+    def flip(values, bit):
+        return lax.ppermute(
+            values, "ctx", [(i, i ^ (1 << bit)) for i in range(ctx_size)]
+        )
+
+    def hop(values, step):
+        return lax.ppermute(
+            values,
+            "ctx",
+            [
+                (2 * order[at] + c, 2 * order[(at + step) % chips] + c)
+                for at in range(chips)
+                for c in range(2)
+            ],
+        )
+
+    def ring_gather(values):
+        right = left = values
+        kept = [values]
+        for step in range(1, chips // 2 + 1):
+            right = hop(right, 1)
+            kept.append(right)
+            if step <= (chips - 1) // 2:
+                left = hop(left, -1)
+                kept.append(left)
+        return [part for mine in kept for part in (mine, flip(mine, 0))]
+
+    def by_shard(mine, others, axis):
+        first = jnp.where(shard == 0, mine, others)
+        second = jnp.where(shard == 0, others, mine)
+        return jnp.concatenate([first, second], axis=axis)
+
+    def gather_small(values, earlier=()):
         if not paired:
             return lax.all_gather(values, "fsdp", axis=0, tiled=True)
-        other = across(values)
-        first = jnp.where(shard == 0, values, other)
-        second = jnp.where(shard == 0, other, values)
-        return jnp.concatenate([first, second], axis=0)
-
-    def fetch(weight):
+        return by_shard(values, across(after(values, *earlier)), 0)
+
+    def fetch(weight, earlier=()):
         if not paired:
-            return [(lax.all_gather(weight, "fsdp", axis=0, tiled=True), 0)]
+            return [(lax.all_gather(weight, "fsdp", axis=0, tiled=True), 0, 0)]
         size = weight.shape[0]
         half = size // 2
-        mine = across(lax.dynamic_slice_in_dim(weight, core * half, half, 0))
-        theirs = core_swap(mine)
-        other = (1 - shard) * size
+        send = after(lax.dynamic_slice_in_dim(weight, core * half, half, 0), *earlier)
+        mine = across(send)
         return [
-            (weight, shard * size),
-            (mine, other + core * half),
-            (theirs, other + (1 - core) * half),
+            (weight, shard * size, 0),
+            (mine, other * size + core * half, 0),
+            (flip(mine, 0), other * size + (1 - core) * half, 0),
         ]
+
+    def fetch_four(weight, parts, earlier):
+        if not paired:
+            return [(lax.all_gather(weight, "fsdp", axis=0, tiled=True), 0, 0)]
+        size, length = weight.shape
+        side = me % 4
+        quarter = length // 4
+        deep = size // parts
+        blocks = [(weight, shard * size, 0)]
+        starts = [(side ^ k) * quarter for k in range(4)]
+        for part in range(parts):
+            send = lax.dynamic_slice(
+                weight, (part * deep, starts[0]), (deep, quarter)
+            )
+            got = across(after(send, *earlier))
+            earlier = (got,)
+            beside = flip(got, 1)
+            row = other * size + part * deep
+            four = [got, flip(got, 0), beside, flip(beside, 0)]
+            blocks += [(four[k], row, starts[k]) for k in range(4)]
+        return blocks
 
     def scatter_sum(values, dim):
         if not paired:
@@ -425,20 +647,48 @@
             )
         half = values.shape[dim] // 2
         keep = lax.dynamic_slice_in_dim(values, shard * half, half, dim)
-        send = lax.dynamic_slice_in_dim(values, (1 - shard) * half, half, dim)
+        send = lax.dynamic_slice_in_dim(values, other * half, half, dim)
         return (keep + across(send.astype(BF16)).astype(F32)).astype(BF16)
 
     def gather(values):
         return lax.all_gather(values, "ctx", axis=0, tiled=False)
+
+    bits = ctx_size.bit_length() - 1
+
+    def halve(values, axis, mine, send):
+        keep = lax.dynamic_index_in_dim(values, mine, axis, keepdims=False)
+        give = lax.dynamic_index_in_dim(values, 1 - mine, axis, keepdims=False)
+        return keep + send(give.astype(BF16)).astype(F32)
+
+    def scatter_rows(values):
+        length = values.shape[1]
+        deep = values.shape[0] // (ctx_size * fsdp_size)
+        values = values.reshape(fsdp_size, -1, 2, deep, length)
+        values = halve(values, 2, core, lambda v: flip(v, 0))
+        if paired:
+            values = halve(values, 0, shard, across)[None]
+        for bit in range(1, bits):
+            values = values.reshape(values.shape[0], -1, 2, deep, length)
+            values = halve(
+                values, 2, (me >> bit) % 2, lambda v, bit=bit: flip(v, bit)
+            )
+        values = values.reshape(-1, deep, length)
+        if not paired:
+            values = lax.psum_scatter(
+                values.astype(BF16), "fsdp", scatter_dimension=0, tiled=True
+            )
+        return values.reshape(deep, length).astype(BF16)
 
     ends = []
     for s in range(seq_count):
         ends.append(lengths[0, s] + (ends[-1] if ends else 0))
     ends_vector = jnp.stack(ends)
+    base = place * rows
     index = me * rows + jnp.arange(rows, dtype=jnp.int32)
     segment = segments(ends, index)
+    seg_col = segment[:, None]
     live = (segment < seq_count).astype(F32)[:, None]
-    all_index = jnp.arange(count, dtype=jnp.int32)
+    all_index = (base[:, None] + jnp.arange(rows, dtype=jnp.int32)[None, :]).reshape(-1)
     all_position = positions(ends, all_index, segments(ends, all_index))
     half_width = head_size // 2
     inverse = jnp.exp(
@@ -448,29 +698,28 @@
     cos = jnp.cos(angle)
     sin = jnp.sin(angle)
 
-    all_tokens = gather(tokens[0]).reshape(count, width)
+    all_tokens = jnp.concatenate(ring_gather(tokens[0]), axis=0)
     inputs = tokens[0].astype(F32)
     grad_y = cotangent[0].astype(F32) * live
     grad_y_b = grad_y.astype(BF16)
     all_grad_y = gather(grad_y_b).reshape(count, width)
 
-    small = [gain_one, bias_one, gain_two, bias_two, bias_down, bias_up]
-    packed = gather_small(jnp.concatenate(small)[None, :])
+    steps_row = time_steps.reshape(1, seq_count)
+    high = (steps_row // 256).astype(BF16)
+    low = (steps_row % 256).astype(BF16)
+    small = [v[None, :] for v in (gain_one, bias_one, gain_two, bias_two, bias_down, bias_up)]
+    packed = gather_small(jnp.concatenate(small + [high, low], axis=1))
     vectors = []
     at = 0
     for vector in small:
-        size = vector.shape[0]
+        size = vector.shape[1]
         vectors.append(packed[:, at : at + size].reshape(1, -1).astype(F32))
         at += size
     gain_first, bias_first, gain_second, bias_second, bias_output, bias_hidden = vectors
-
-    all_steps = lax.all_gather(time_steps.astype(F32), "fsdp", axis=0, tiled=True)
+    all_steps = packed[:, at : at + seq_count].astype(F32) * 256.0 + packed[
+        :, at + seq_count :
+    ].astype(F32)
     all_embedded = embed(all_steps, w_time.shape[0] * fsdp_size).astype(BF16)
-    embedded = lax.dynamic_index_in_dim(all_embedded, shard, 0, keepdims=False)
-    film = times_rows(embedded, fetch(w_time))
-    film = jnp.concatenate([film, jnp.zeros((1, 2 * width), F32)], axis=0)
-    gains = gain_first + film[:, :width]
-    shifts = bias_first + film[:, width:]
 
     head = me // repeats
     w_head = jnp.concatenate(
@@ -481,65 +730,161 @@
         + [jnp.zeros((w_qkv.shape[0], head_size), BF16)],
         axis=1,
     )
-    w_head = gather_small(w_head)
-
-    base = jnp.arange(ctx_size, dtype=jnp.int32) * rows
+    w_head = gather_small(w_head, (packed,))
+
+    if paired:
+        other_grad_y = across(after(grad_y_b, w_head))
+        time_blocks = fetch(w_time, (other_grad_y,))
+        grad_act_part = dims(
+            jnp.concatenate([grad_y_b, other_grad_y], axis=0), w_down, 1, 1
+        )
+        grad_act_send = after(grad_act_part[rows:].astype(BF16), time_blocks[1][0])
+        grad_act_got = across(grad_act_send)
+        grad_act = by_shard(grad_act_part[:rows], grad_act_got.astype(F32), 1)
+        out_blocks = fetch(w_out, (grad_act_got,))
+        up_blocks = fetch_four(w_up, 2, (out_blocks[1][0],))
+        slice_width = hidden // (ctx_size * fsdp_size)
+        other_rows = across(
+            after(
+                lax.dynamic_slice_in_dim(w_down, me * slice_width, slice_width, 0),
+                up_blocks[-4][0],
+            )
+        )
+        own_rows = lax.dynamic_slice_in_dim(w_down, me * slice_width, slice_width, 0)
+        w_down_slice = by_shard(own_rows, other_rows, 0)
+        qkv_blocks = fetch(w_qkv, (other_rows,))
+        down_blocks = fetch(w_down, (qkv_blocks[1][0],))
+    else:
+        time_blocks = fetch(w_time)
+        out_blocks = fetch(w_out)
+        up_blocks = fetch(w_up)
+        down_blocks = fetch(w_down)
+        qkv_blocks = fetch(w_qkv)
+        grad_act = times_t(grad_y_b, down_blocks, hidden)
+        slice_width = hidden // (ctx_size * fsdp_size)
+        full_down = down_blocks[0][0].reshape(fsdp_size, ctx_size, slice_width, width)
+        w_down_slice = lax.dynamic_index_in_dim(full_down, me, 1, keepdims=False)
+        w_down_slice = w_down_slice.reshape(-1, width)
+
+    embedded = lax.dynamic_index_in_dim(all_embedded, shard, 0, keepdims=False)
+    film = times(embedded.reshape(seq_count, -1), time_blocks, 2 * width)
+    film = jnp.concatenate([film, jnp.zeros((1, 2 * width), F32)], axis=0)
+    gains = gain_first + film[:, :width]
+    shifts = bias_first + film[:, width:]
+
     all_norm, query_t, key, key_t, value_t, pair = project(
         all_tokens, base, ends_vector, gains, shifts, w_head, cos, sin, rows, head_size
     )
-    out_t, sent, lse = attend(query_t, key, value_t, rows)
-
+    out_t, sent, lse = attend(place, query_t, key, value_t, rows)
     part = (me % repeats) * columns
     if repeats > 1:
         sent = lax.dynamic_slice_in_dim(sent, part, columns, 1)
     attended_t = lax.all_to_all(sent, "ctx", 0, 0, tiled=True).reshape(width, rows)
 
-    out_pieces = fetch(w_out)
-    up_pieces = fetch(w_up)
-    down_pieces = fetch(w_down)
-    qkv_pieces = fetch(w_qkv)
-    resid = inputs + times_rows_t(attended_t, out_pieces)
+    resid = inputs + sum(
+        dims(lax.dynamic_slice_in_dim(attended_t, row, b.shape[0], 0), b, 0, 0)
+        for b, row, _ in out_blocks
+    )
     normal_two, scale_two = stats(resid)
     norm_two_b = (normal_two * gain_second + bias_second).astype(BF16)
     all_norm_two = gather(norm_two_b).reshape(count, width)
-    pre = times_rows(norm_two_b, up_pieces) + bias_hidden
+    pre = times(norm_two_b, up_blocks, hidden) + bias_hidden
     act, slope = gelu_parts(pre)
-    branch = times_rows(act.astype(BF16), down_pieces) + bias_output
-    output = (live * (resid + branch)).astype(BF16)
-    grad_act = joined([dims(grad_y_b, p, 1, 1) for p, _ in down_pieces], down_pieces, 1)
+    act_b = act.astype(BF16)
     grad_pre = grad_act * slope
     grad_bias_up = jnp.sum(grad_pre, axis=0)
     grad_pre_b = grad_pre.astype(BF16)
-    grad_norm_two = joined([dims(grad_pre_b, p, 1, 1) for p, _ in up_pieces], up_pieces, 1)
+    grad_norm_two = times_t(grad_pre_b, up_blocks, width)
     grad_resid = grad_y + stats_back(grad_norm_two * gain_second, normal_two, scale_two)
     grad_resid_b = grad_resid.astype(BF16)
-    grad_att_t = joined(
-        [dims(p, grad_resid_b, 1, 1) for p, _ in out_pieces], out_pieces, 0
-    ).astype(BF16)
-    grad_att_t = grad_att_t.reshape(HEADS, head_size, rows)
+    if len(out_blocks) == 1:
+        grad_att_t = dims(out_blocks[0][0], grad_resid_b, 1, 1)
+    else:
+        grad_att_t = jnp.zeros((width, rows), F32)
+        for b, row, _ in out_blocks:
+            grad_att_t = lax.dynamic_update_slice_in_dim(
+                grad_att_t, dims(b, grad_resid_b, 1, 1), row, 0
+            )
+    grad_att_t = grad_att_t.astype(BF16).reshape(HEADS, head_size, rows)
     if repeats > 1:
         grad_att_t = jnp.repeat(grad_att_t, repeats, axis=0)
     grad_att = lax.all_to_all(grad_att_t, "ctx", 0, 0, tiled=True)
 
-    mixed_t = attend_back(
-        query_t, grad_att, out_t, lse, key, key_t, pair, cos, sin, rows
-    )
-    mixed_t = mixed_t.reshape(3, head_size, count)
+    mixed_t, mixed_sent = attend_back(
+        place, query_t, grad_att, out_t, lse, key, key_t, pair, cos, sin, rows
+    )
     if repeats > 1:
+        mixed_t = mixed_t.reshape(3, head_size, count)
         mixed_t = lax.dynamic_slice_in_dim(mixed_t, part, columns, 1)
-    mixed_t = mixed_t.reshape(3 * columns, count)
-    mixed_sent = mixed_t.reshape(3 * columns, ctx_size, rows).transpose(1, 0, 2)
+        mixed_t = mixed_t.reshape(3 * columns, count)
+        mixed_sent = mixed_sent.reshape(ctx_size, 3, head_size, rows)
+        mixed_sent = lax.dynamic_slice_in_dim(mixed_sent, part, columns, 2)
+        mixed_sent = mixed_sent.reshape(ctx_size, 3 * columns, rows)
     mixed_got = lax.all_to_all(mixed_sent, "ctx", 0, 0, tiled=True)
     grad_mixed_t = (
         mixed_got.reshape(ctx_size, 3, columns, rows)
         .transpose(1, 0, 2, 3)
         .reshape(3 * width, rows)
     )
-    grad_norm_one = joined(
-        [dims(grad_mixed_t, p, 0, 1) for p, _ in qkv_pieces], qkv_pieces, 1
-    )
+
+    starts = [k * (hidden // fsdp_size) + me * slice_width for k in range(fsdp_size)]
+    w_up_slice = jnp.concatenate(
+        [columns_of(up_blocks, start, slice_width, width) for start in starts], axis=1
+    )
+    bias_slice = jnp.concatenate(
+        [
+            lax.dynamic_slice_in_dim(bias_hidden, start, slice_width, 1)
+            for start in starts
+        ],
+        axis=1,
+    )
+    pre_slice = dims(all_norm_two, w_up_slice, 1, 0) + bias_slice
+    act_slice, slope_slice = gelu_parts(pre_slice)
+    grad_pre_slice = (dims(all_grad_y, w_down_slice, 1, 1) * slope_slice).astype(BF16)
+    down_slice = scatter_sum(dims(act_slice.astype(BF16), all_grad_y, 0, 0), 0)
+    up_slice = scatter_sum(dims(all_norm_two, grad_pre_slice, 0, 0), 0)
+    packable = paired and slice_width == 128
+    if packable:
+        sliced = jnp.concatenate(
+            [up_slice[:, k * 128 : (k + 1) * 128] for k in range(fsdp_size)]
+            + [down_slice[:, k * 128 : (k + 1) * 128] for k in range(width // 128)],
+            axis=0,
+        )
+        sliced = gather(sliced)
+        grad_up = expand_up(sliced, width // fsdp_size, fsdp_size)
+        grad_down = expand_down(sliced, width)
+    else:
+        grad_down = gather(down_slice).reshape(-1, width).astype(F32)
+        grad_up = (
+            gather(up_slice)
+            .reshape(ctx_size, width // fsdp_size, fsdp_size, slice_width)
+            .transpose(1, 2, 0, 3)
+            .reshape(width // fsdp_size, hidden)
+            .astype(F32)
+        )
+
+    out_rows = scatter_rows(jnp.dot(attended_t, grad_resid_b, preferred_element_type=F32))
+    qkv_slice = scatter_sum(jnp.dot(mixed_t, all_norm, preferred_element_type=F32), 1)
+    if packable and repeats == 1:
+        deep = width // fsdp_size
+        last = jnp.concatenate(
+            [qkv_slice] + [out_rows[:, k * deep : (k + 1) * deep] for k in range(fsdp_size)],
+            axis=0,
+        )
+        last = jnp.stack(ring_gather(last))
+        grad_qkv, grad_out = expand_last(place, where, last, width, head_size)
+    else:
+        grad_out = gather(out_rows).reshape(-1, width).astype(F32)
+        grad_qkv = (
+            gather(qkv_slice)
+            .reshape(ctx_size, 3, columns, width // fsdp_size)
+            .transpose(3, 1, 0, 2)
+            .reshape(width // fsdp_size, 3 * width)
+            .astype(F32)
+        )
+
+    grad_norm_one = times_t(grad_mixed_t.T, qkv_blocks, width)
     normal_one, scale_one = stats(inputs)
-    seg_col = segment[:, None]
     gain_tok = gains[0:1]
     for s in range(1, seq_count + 1):
         gain_tok = jnp.where(seg_col == s, gains[s : s + 1], gain_tok)
@@ -551,6 +896,8 @@
         jnp.sum(jnp.where(seg_col == s, film_terms, 0.0), axis=0)
         for s in range(seq_count + 1)
     ]
+    branch = times(act_b, down_blocks, width) + bias_output
+    output = (live * (resid + branch)).astype(BF16)
 
     sums = [
         jnp.sum(grad_norm_two * normal_two, axis=0),
@@ -559,8 +906,10 @@
         grad_bias_up,
     ] + film_sums
     sizes = [vector.shape[0] for vector in sums]
-    total = lax.psum(jnp.concatenate(sums)[None, :], "ctx")
-    total = lax.all_gather(total, "fsdp", axis=0, tiled=True)
+    total = jnp.concatenate(sums)[None, :]
+    for bit in range(bits):
+        total = total + flip(total, bit)
+    total = gather_small(total)
     split = []
     at = 0
     for size in sizes:
@@ -587,59 +936,6 @@
     grad_time = sum(
         embedded_rows[g][:, None] * film_grad[g][None, :]
         for g in range(film_grad.shape[0])
-    )
-
-    slice_width = hidden // (ctx_size * fsdp_size)
-    starts = [
-        k * (hidden // fsdp_size) + me * slice_width for k in range(fsdp_size)
-    ]
-    w_up_cols = []
-    for piece, _ in up_pieces:
-        w_up_cols.append(
-            jnp.concatenate(
-                [
-                    lax.dynamic_slice_in_dim(piece, start, slice_width, 1)
-                    for start in starts
-                ],
-                axis=1,
-            )
-        )
-    w_up_slice = joined(w_up_cols, up_pieces, 0)
-    w_down_slice = jnp.concatenate(
-        [rows_of(down_pieces, start, slice_width) for start in starts], axis=0
-    )
-    bias_slice = jnp.concatenate(
-        [
-            lax.dynamic_slice_in_dim(bias_hidden, start, slice_width, 1)
-            for start in starts
-        ],
-        axis=1,
-    )
-    pre_slice = dims(all_norm_two, w_up_slice, 1, 0) + bias_slice
-    act_slice, slope_slice = gelu_parts(pre_slice)
-    grad_pre_slice = (dims(all_grad_y, w_down_slice, 1, 1) * slope_slice).astype(BF16)
-    down_slice = dims(act_slice.astype(BF16), all_grad_y, 0, 0)
-    up_slice = dims(all_norm_two, grad_pre_slice, 0, 0)
-    grad_down = gather(scatter_sum(down_slice, 0)).reshape(-1, width).astype(F32)
-    up_parts = gather(scatter_sum(up_slice, 0))
-    grad_up = (
-        up_parts.reshape(ctx_size, width // fsdp_size, fsdp_size, slice_width)
-        .transpose(1, 2, 0, 3)
-        .reshape(width // fsdp_size, hidden)
-        .astype(F32)
-    )
-    out_part = jnp.dot(attended_t, grad_resid_b, preferred_element_type=F32)
-    out_rows = lax.psum_scatter(
-        out_part.astype(BF16), ("fsdp", "ctx"), scatter_dimension=0, tiled=True
-    )
-    grad_out = gather(out_rows).reshape(-1, width).astype(F32)
-    qkv_slice = jnp.dot(mixed_t, all_norm, preferred_element_type=F32)
-    qkv_parts = gather(scatter_sum(qkv_slice, 1))
-    grad_qkv = (
-        qkv_parts.reshape(ctx_size, 3, columns, width // fsdp_size)
-        .transpose(3, 1, 0, 2)
-        .reshape(width // fsdp_size, 3 * width)
-        .astype(F32)
     )
     return (
         output[None],

time: 667 us -> 452 us (0.68)
  waiting for transfers between devices: 278 us -> 152 us
  blocking collectives: 120 us -> 0 us
  starting transfers between devices: 28.8 us -> 73 us
  Pallas kernels: 40.4 us -> 64.3 us
  matrix products: 75.1 us -> 51.9 us
  local copies, waits for them, and re-layouts: 72.9 us -> 57.7 us
    reduce_scatter x1 -> x0, waiting for transfers between devices: 124 us -> none  [body(): lax.psum_scatter(out_part.astype(BF16), ('fsdp', 'ctx'), scatter_dimensio...]
    psum x1 -> x0, blocking collectives: 59.8 us -> none  [body(): total = lax.psum(jnp.concatenate(sums)[None, :], 'ctx')]
    ppermute x5 -> x48, waiting for transfers between devices: 0.01 us -> 57.6 us  [the longest x34 41.8 us: flip(): lax.ppermute(values, 'ctx', [(i, i ^ 1 << bit) for i in range(ctx_size)])]
    unnamed x1 -> x0, blocking collectives: 55.6 us -> none
    all_gather x7 -> x3, waiting for transfers between devices: 63.6 us -> 26.6 us  [gather(): return lax.all_gather(values, 'ctx', axis=0, tiled=False)]
    ppermute x10 -> x16, waiting for transfers between devices: 83.8 us -> 51.5 us  [across(): return lax.ppermute(values, 'fsdp', [(0, 1), (1, 0)])]
    ppermute x5 -> x48, starting transfers between devices: 0.64 us -> 30.3 us  [the longest x14 16.2 us: hop(): lax.ppermute(values, 'ctx', [(2 * order[at] + c, 2 * order[(at + step) %...]
    convert_element_type x3 -> x5, local copies, waits for them, and re-layouts: 22.9 us -> 0.29 us  [halve(): return keep + send(give.astype(BF16)).astype(F32)]
  transfers between devices with their start and end apart: 26 -> 70, of which waited for: 9 -> 23; matrix products, arithmetic and copies ran while one was open for 23% -> 29% of each run, Pallas kernels for 6% -> 12%
where the time goes in v2:
time: 452 us; the launch traced here: 443 us
  waiting for transfers between devices  152 us (34%)
  starting transfers between devices  73 us (16%)
  Pallas kernels  64.3 us (14%)
  local copies, waits for them, and re-layouts  57.7 us (13%)
  matrix products  51.9 us (11%)
  other arithmetic  27.2 us (6%)
  between operations  16.8 us (4%)
    ppermute x16, waiting for transfers between devices, across(): return lax.ppermute(values, 'fsdp', [(0, 1), (1, 0)])  51.5 us
    ppermute x34, waiting for transfers between devices, flip(): lax.ppermute(values, 'ctx', [(i, i ^ 1 << bit) for i in range(ctx_size)])  41.8 us
    dot_general x22, matrix products, dims(): lax.dot_general(left, right, (((left_dim,), (right_dim,)), ((), ())), pre...  37 us
    all_gather x3, waiting for transfers between devices, gather(): return lax.all_gather(values, 'ctx', axis=0, tiled=False)  26.6 us
    unnamed x126, local copies, waits for them, and re-layouts  25.8 us
    ppermute x16, starting transfers between devices, across(): return lax.ppermute(values, 'fsdp', [(0, 1), (1, 0)])  19.8 us
    pallas_call x1, Pallas kernels, attend_back(): pl.pallas_call(functools.partial(attend_back_kernel, chunk, rows, head_si...  19.1 us
    ppermute x14, starting transfers between devices, hop(): lax.ppermute(values, 'ctx', [(2 * order[at] + c, 2 * order[(at + step) %...  16.2 us
  transfers between devices with their start and end apart: 70, of which 23 were waited for; matrix products, arithmetic and copies ran while one was open for 29% of the time, Pallas kernels for 12%

profile of v2, /device:TPU:0, one launch (start us, length us, event | category | flops | bytes accessed | tf_op | source)
XLA Modules:
  0.0 443.4 jit_solution(4453793798725593707)
XLA Ops:
  7.2 3.1 collective-permute-start.1
  12.5 1.9 collective-permute-start.16
  19.5 1.7 constant_dynamic-update-slice_fusion.15
  24.7 1.8 multiply_sine_fusion
  30.5 1.9 collective-permute-start.17
  35.0 1.7 constant_dynamic-update-slice_fusion.14
  36.6 1.7 constant_dynamic-update-slice_fusion.13
  38.5 1.6 collective-permute-start.18
  40.2 3.5 fusion.43
  49.7 2.7 collective-permute-done.9
  58.6 4.0 collective-permute-done.13
  66.1 10.6 %project_head.1 = (bf16[2048,1024]{1,0:T(8,128)(2,1)}, bf16[128,2048]{1,0:T(8,128)(2,1)}, bf16[2048,128]{1,0:T(8,128)(2,1)}, bf16[64,2048]{1,0:T(8,128)(2,1)}, b...) custom-call(s32[1]{0:T(128)} %bitcast.220.ends_ref, s32[16]{0:T(128)} %copy-done.36, ...), custom_call_target="tpu_custom_call" | custom-call | flops 1073741824 | bytes 8388608 | tf_op jit(solution)/shard_map/project_head/pallas_call | solution.py:259
  76.6 13.0 %attend_head.1 = (f32[64,2048]{1,0:T(8,128)}, bf16[16,64,128]{2,1,0:T(8,128)(2,1)}, f32[1,2048]{1,0:T(1,128)}) custom-call(s32[16]{0:T(128)} %fusion.135.place_ref, bf16[128,2048]{1,0:T(8,128)(2,1)} %get-tuple-element.39.query_ref, bf16[2048,128]{1,0:T(8,128)(2,1)} %get-tuple-element.40.key_ref, bf16[64,2048]{1,0:T(8,128)(2,1)} %get-tuple-element.41.value_ref), custom_call_target="tpu_custom_call" | custom-call | flops 4294967296 | bytes 2097152 | tf_op jit(solution)/shard_map/attend_head/pallas_call | solution.py:302
  89.6 6.2 %all-to-all-start = ((bf16[16,64,128]{2,1,0:T(8,128)(2,1)}), bf16[16,64,128]{2,1,0:T(8,128)(2,1)S(1)}, u32[]{:S(2)}, u32[]{:S(2)}) async-start(bf16[16,64,128]{2,1,0:T(8,128)(2,1)} %get-tuple-element.42), calls=%async_computation | async-start | bytes 524288 | tf_op jit(solution)/shard_map/all_to_all | solution.py:782
  96.5 9.5 %all-to-all-done = bf16[16,64,128]{2,1,0:T(8,128)(2,1)S(1)} async-done(((bf16[16,64,128]{2,1,0:T(8,128)(2,1)}), bf16[16,64,128]{2,1,0:T(8,128)(2,1)S(1)}, u32[]{:S(2)}, u32[]{:S(2)}) %all-to-all-start) | async-done | bytes 262176 | tf_op jit(solution)/shard_map/all_to_all | solution.py:782
  109.3 2.7 constant_dynamic-slice_fusion.9
  115.7 3.1 constant_dynamic-slice_fusion.10
  118.8 2.1 constant_dynamic-slice_fusion.11
  121.7 1.7 dynamic-slice_dynamic-update-slice_fusion
  124.1 1.7 dynamic-slice_dynamic-update-slice_fusion.1
  128.0 11.9 %collective-permute-done.23 = bf16[256,1024]{1,0:T(8,128)(2,1)S(1)} collective-permute-done((bf16[256,1024]{1,0:T(8,128)(2,1)}, bf16[256,1024]{1,0:T(8,128)(2,1)S(1)}, u32[]{:S(2)}, u32[]{:S(2)}) %collective-permute-start.23) | collective-permute-done | bytes 524320 | tf_op jit(solution)/shard_map/ppermute | solution.py:570
  141.9 1.7 convert_select_fusion.1
  143.6 9.2 %collective-permute-done.24 = bf16[256,1024]{1,0:T(8,128)(2,1)S(1)} collective-permute-done((bf16[256,1024]{1,0:T(8,128)(2,1)S(1)}, bf16[256,1024]{1,0:T(8,128)(2,1)S(1)}, u32[]{:S(2)}, u32[]{:S(2)}) %collective-permute-start.24) | collective-permute-done | bytes 524320 | tf_op jit(solution)/shard_map/ppermute | solution.py:570
  154.3 1.7 collective-permute-start.28
  156.1 2.3 collective-permute-done.27
  160.8 1.8 broadcast_select_fusion.1
  162.6 6.4 %collective-permute-done.28 = bf16[256,1024]{1,0:T(8,128)(2,1)S(1)} collective-permute-done((bf16[256,1024]{1,0:T(8,128)(2,1)S(1)}, bf16[256,1024]{1,0:T(8,128)(2,1)S(1)}, u32[]{:S(2)}, u32[]{:S(2)}) %collective-permute-start.28) | collective-permute-done | bytes 524320 | tf_op jit(solution)/shard_map/ppermute | solution.py:573
  173.6 3.6 fusion.166
  182.1 4.9 %convolution_add_fusion.1 = f32[2048,256]{1,0:T(8,128)} fusion(bf16[2048,1024]{1,0:T(8,128)(2,1)} %all-gather.8.cloned.1.call-done, f32[256]{0:T(256)S(1)} %bitcast.259, bf16[1024,128]{1,0:T(8,128)(2,1)} %select_dynamic-update-slice_fusion, bf16[1024,128]{1,0:T(8,128)(2,1)} %select_dynamic-update-slice_fusion.2), kind=kOutput, calls=%fused_computation.5 | convolution fusion | flops 1075314688 | bytes 6816768 | tf_op jit(solution)/shard_map/dot_general | solution.py:22
  187.0 26.6 %all-gather.6.cloned.1.call-done = bf16[16,128,1024]{2,1,0:T(8,128)(2,1)} async-done(((bf16[1,128,1024]{2,1,0:T(8,128)(2,1)}), bf16[16,128,1024]{2,1,0:T(8,128)(2,1)}) %all-gather.6.cloned.1.call-update) | async-done | bytes 4194320 | tf_op jit(solution)/shard_map/all_gather | solution.py:654
  213.6 9.6 %fusion.25 = f32[1024,256]{1,0:T(8,128)} fusion(bf16[2048,1024]{1,0:T(8,128)(2,1)} %all-gather.8.cloned.1.call-done, bf16[2048,1024]{1,0:T(8,128)(2,1)} %bitcast.260, f32[2048,256]{1,0:T(8,128)} %convolution_add_fusion.1, bf16[128,1024]{1,0:T(8,128)(2,1)S(1)} %copy-done.22, bf16[128,1024]{1,0:T(8,128)(2,1)S(1)} %get-tuple-element.84), kind=kOutput, calls=%fused_computation.68 | convolution fusion | flops 2153775104 | bytes 12058624 | tf_op jit(solution)/shard_map/dot_general | solution.py:22
  225.8 4.1 fusion.24
  230.6 2.3 collective-permute-done.57
  234.3 4.1 collective-permute-done.58
  243.4 1.7 fusion.168
  246.5 2.0 copy-done.2
  252.0 12.6 %all-to-all-start.1 = ((bf16[16,64,128]{2,1,0:T(8,128)(2,1)}), bf16[16,64,128]{2,1,0:T(8,128)(2,1)S(1)}, u32[]{:S(2)}, u32[]{:S(2)}) async-start(bf16[16,64,128]{2,1,0:T(8,128)(2,1)} %bitcast.21), calls=%async_computation.1 | async-start | bytes 524288 | tf_op jit(solution)/shard_map/all_to_all | solution.py:811
  264.6 2.3 bitcast_add_fusion
  269.8 7.2 %all-to-all-done.1.grad_ref = bf16[16,64,128]{2,1,0:T(8,128)(2,1)S(1)} async-done(((bf16[16,64,128]{2,1,0:T(8,128)(2,1)}), bf16[16,64,128]{2,1,0:T(8,128)(2,1)S(1)}, u32[]{:S(2)}, u32[]{:S(2)}) %all-to-all-start.1) | async-done | bytes 262176 | tf_op jit(solution)/shard_map/all_to_all | solution.py:811
  277.7 19.1 %attend_head_back.1 = (bf16[192,2048]{1,0:T(8,128)(2,1)}, bf16[16,192,128]{2,1,0:T(8,128)(2,1)}) custom-call(s32[16]{0:T(128)} %fusion.135.place_ref, bf16[128,2048]{1,0:T(8,128)(2,1)} %get-tuple-element.39.query_ref, bf16[16,64,128]{2,1,0:T(8,128)(2,1)} %copy-done.23, f32[64,2048]{1,0:T(8,128)} %get-tuple-element.50.out_ref, ...), custom_call_target="tpu_custom_call" | custom-call | flops 10737418240 | bytes 4194304 | tf_op jit(solution)/shard_map/attend_head_back/pallas_call | solution.py:351
  296.8 3.8 all-to-all-start.2
  302.2 1.9 collective-permute-start.39
  304.0 3.2 fusion.174
  308.7 6.6 %collective-permute-done.39 = bf16[1,4,32,1024]{3,2,1,0:T(8,128)(2,1)S(1)} collective-permute-done((bf16[1,4,32,1024]{3,2,1,0:T(8,128)(2,1)S(1)}, bf16[1,4,32,1024]{3,2,1,0:T(8,128)(2,1)S(1)}, u32[]{:S(2)}, u32[]{:S(2)}) %collective-permute-start.39) | collective-permute-done | bytes 262176 | tf_op jit(solution)/shard_map/ppermute | solution.py:573
  316.0 14.4 %collective-permute-done.40 = bf16[1,2,32,1024]{3,2,1,0:T(8,128)(2,1)S(1)} collective-permute-done((bf16[1,2,32,1024]{3,2,1,0:T(8,128)(2,1)S(1)}, bf16[1,2,32,1024]{3,2,1,0:T(8,128)(2,1)S(1)}, u32[]{:S(2)}, u32[]{:S(2)}) %collective-permute-start.40) | collective-permute-done | bytes 131104 | tf_op jit(solution)/shard_map/ppermute | solution.py:573
  330.5 3.1 collective-permute-start.41
  333.8 3.1 convolution_dynamic-update-slice_fusion
  336.9 2.1 convolution_dynamic-update-slice_fusion.3
  339.7 2.4 convolution_dynamic-update-slice_fusion.2
  344.8 1.7 collective-permute-start.33
  348.6 1.9 collective-permute-done.60
  352.3 5.2 %collective-permute-done.61 = f32[1,11264]{1,0:T(1,128)S(1)} collective-permute-done((f32[1,11264]{1,0:T(1,128)S(1)}, f32[1,11264]{1,0:T(1,128)S(1)}, u32[]{:S(2)}, u32[]{:S(2)}) %collective-permute-start.61) | collective-permute-done | bytes 45088 | tf_op jit(solution)/shard_map/ppermute | solution.py:573
  359.2 3.4 collective-permute-done.62
  362.6 3.0 collective-permute-start.49
  366.6 3.4 collective-permute-done.49
  370.0 23.6 %collective-permute-done.63 = f32[1,11264]{1,0:T(1,128)S(1)} collective-permute-done((f32[1,11264]{1,0:T(1,128)S(1)}, f32[1,11264]{1,0:T(1,128)S(1)}, u32[]{:S(2)}, u32[]{:S(2)}) %collective-permute-start.63) | collective-permute-done | bytes 45088 | tf_op jit(solution)/shard_map/ppermute | solution.py:570
  393.6 1.8 collective-permute-start.53
  402.0 2.0 convolution_add_fusion.3
  404.0 5.3 %collective-permute-done.55 = bf16[256,512]{1,0:T(8,128)(2,1)S(1)} collective-permute-done((bf16[256,512]{1,0:T(8,128)(2,1)S(1)}, bf16[256,512]{1,0:T(8,128)(2,1)S(1)}, u32[]{:S(2)}, u32[]{:S(2)}) %collective-permute-start.55) | collective-permute-done | bytes 262176 | tf_op jit(solution)/shard_map/ppermute | solution.py:578
  410.9 2.0 copy-done.7
  412.9 9.3 %expand_last.1 = (f32[512,3072]{1,0:T(8,128)}, f32[512,1024]{1,0:T(8,128)}) custom-call(s32[16]{0:T(128)} %fusion.135.place_ref, s32[8]{0:T(128)} %fusion.150.where_ref, bf16[16,256,512]{2,1,0:T(8,128)(2,1)} %copy-done.7), custom_call_target="tpu_custom_call" | custom-call | tf_op jit(solution)/shard_map/expand_last/pallas_call | solution.py:443
  422.2 2.1 fusion.20
  424.3 6.2 %expand_up.1 = f32[512,4096]{1,0:T(8,128)} custom-call(bf16[16,2048,128]{2,1,0:T(8,128)(2,1)} %bitcast.221), custom_call_target="tpu_custom_call" | custom-call | tf_op jit(solution)/shard_map/expand_up/pallas_call | solution.py:385
  430.5 6.2 %expand_down.1 = f32[2048,1024]{1,0:T(8,128)} custom-call(bf16[16,2048,128]{2,1,0:T(8,128)(2,1)} %bitcast.222), custom_call_target="tpu_custom_call" | custom-call | tf_op jit(solution)/shard_map/expand_down/pallas_call | solution.py:399
  (367 shorter events, 98.1 us)
Async XLA Ops:
  7.2 25.1 %collective-permute-start.1 = (bf16[128,1024]{1,0:T(8,128)(2,1)}, bf16[128,1024]{1,0:T(8,128)(2,1)}, u32[]{:S(2)}, u32[]{:S(2)}) collective-permute-start(bf16[128,1024]{1,0:T(8,128)(2,1)} %bitcast.226), channel_id=1, source_target_pairs={{0,8},{2,10},{8,16},{10,18},{16,24},{18,26},{24,28},{26,30},{28,20... | collective-permute-start | bytes 786440 | tf_op jit(solution)/shard_map/ppermute | solution.py:578
  10.3 24.2 %collective-permute-start = (bf16[128,1024]{1,0:T(8,128)(2,1)}, bf16[128,1024]{1,0:T(8,128)(2,1)}, u32[]{:S(2)}, u32[]{:S(2)}) collective-permute-start(bf16[128,1024]{1,0:T(8,128)(2,1)} %bitcast.227), channel_id=1, source_target_pairs={{0,2},{2,0},{4,6},{6,4},{8,10},{10,8},{12,14},{14,12},{16,18},{18,... | collective-permute-start | bytes 786440 | tf_op jit(solution)/shard_map/ppermute | solution.py:573
  10.3 23.7 %collective-permute-start.3 = (bf16[128,1024]{1,0:T(8,128)(2,1)}, bf16[128,1024]{1,0:T(8,128)(2,1)S(1)}, u32[]{:S(2)}, u32[]{:S(2)}) collective-permute-start(bf16[128,1024]{1,0:T(8,128)(2,1)} %bitcast.228), channel_id=1, source_target_pairs={{0,4},{2,6},{8,0},{10,2},{16,8},{18,10},{24,16},{26,18},{28,24},{3... | collective-permute-start | bytes 786440 | tf_op jit(solution)/shard_map/ppermute | solution.py:578
  12.5 15.9 %collective-permute-start.16 = (bf16[512,256]{1,0:T(8,128)(2,1)}, bf16[512,256]{1,0:T(8,128)(2,1)}, u32[]{:S(2)}, u32[]{:S(2)}) collective-permute-start(bf16[512,256]{1,0:T(8,128)(2,1)} %maximum_maximum_fusion), channel_id=1, source_target_pairs={{0,1},{1,0},{2,3},{3,2},{4,5},{5,4},{6,7},{7,6},{8,9},{9,8},{10,11... | collective-permute-start | bytes 786440 | tf_op jit(solution)/shard_map/ppermute | solution.py:570
  19.3 8.5 %collective-permute-start.15 = (bf16[1,4610]{1,0:T(2,128)(2,1)S(1)}, bf16[1,4610]{1,0:T(2,128)(2,1)S(1)}, u32[]{:S(2)}, u32[]{:S(2)}) collective-permute-start(bf16[1,4610]{1,0:T(2,128)(2,1)S(1)} %concatenate.69), channel_id=1, source_target_pairs={{0,1},{1,0},{2,3},{3,2},{4,5},{5,4},{6,7},{7,6},{8,9},{9,8},{10,11... | collective-permute-start | bytes 27668 | tf_op jit(solution)/shard_map/ppermute | solution.py:570
  30.5 8.1 %collective-permute-start.17 = (bf16[128,1024]{1,0:T(8,128)(2,1)S(1)}, bf16[128,1024]{1,0:T(8,128)(2,1)S(1)}, u32[]{:S(2)}, u32[]{:S(2)}) collective-permute-start(bf16[128,1024]{1,0:T(8,128)(2,1)S(1)} %fusion.40), channel_id=1, source_target_pairs={{0,1},{1,0},{2,3},{3,2},{4,5},{5,4},{6,7},{7,6},{8,9},{9,8},{10,11... | collective-permute-start | bytes 786440 | tf_op jit(solution)/shard_map/ppermute | solution.py:570
  32.3 7.9 %collective-permute-start.5 = (bf16[128,1024]{1,0:T(8,128)(2,1)}, bf16[128,1024]{1,0:T(8,128)(2,1)S(1)}, u32[]{:S(2)}, u32[]{:S(2)}) collective-permute-start(bf16[128,1024]{1,0:T(8,128)(2,1)} %collective-permute-done.1), channel_id=1, source_target_pairs={{0,8},{2,10},{8,16},{10,18},{16,24},{18,26},{24,28},{26,30},{28,20... | collective-permute-start | bytes 786440 | tf_op jit(solution)/shard_map/ppermute | solution.py:578
  33.9 9.8 %collective-permute-start.2 = (bf16[128,1024]{1,0:T(8,128)(2,1)}, bf16[128,1024]{1,0:T(8,128)(2,1)S(1)}, u32[]{:S(2)}, u32[]{:S(2)}) collective-permute-start(bf16[128,1024]{1,0:T(8,128)(2,1)} %collective-permute-done.1), channel_id=1, source_target_pairs={{0,2},{2,0},{4,6},{6,4},{8,10},{10,8},{12,14},{14,12},{16,18},{18,... | collective-permute-start | bytes 786440 | tf_op jit(solution)/shard_map/ppermute | solution.py:573
  34.0 13.0 %collective-permute-start.4 = (bf16[128,1024]{1,0:T(8,128)(2,1)S(1)}, bf16[128,1024]{1,0:T(8,128)(2,1)S(1)}, u32[]{:S(2)}, u32[]{:S(2)}) collective-permute-start(bf16[128,1024]{1,0:T(8,128)(2,1)S(1)} %collective-permute-done.3), channel_id=1, source_target_pairs={{0,2},{2,0},{4,6},{6,4},{8,10},{10,8},{12,14},{14,12},{16,18},{18,... | collective-permute-start | bytes 786440 | tf_op jit(solution)/shard_map/ppermute | solution.py:573
  34.5 10.8 %collective-permute-start.7 = (bf16[128,1024]{1,0:T(8,128)(2,1)S(1)}, bf16[128,1024]{1,0:T(8,128)(2,1)S(1)}, u32[]{:S(2)}, u32[]{:S(2)}) collective-permute-start(bf16[128,1024]{1,0:T(8,128)(2,1)S(1)} %collective-permute-done.3), channel_id=1, source_target_pairs={{0,4},{2,6},{8,0},{10,2},{16,8},{18,10},{24,16},{26,18},{28,24},{3... | collective-permute-start | bytes 786440 | tf_op jit(solution)/shard_map/ppermute | solution.py:578
  38.5 10.4 %collective-permute-start.18 = (bf16[64,2048]{1,0:T(8,128)(2,1)S(1)}, bf16[64,2048]{1,0:T(8,128)(2,1)S(1)}, u32[]{:S(2)}, u32[]{:S(2)}) collective-permute-start(bf16[64,2048]{1,0:T(8,128)(2,1)S(1)} %constant_dynamic-slice_fusion.17), channel_id=1, source_target_pairs={{0,1},{1,0},{2,3},{3,2},{4,5},{5,4},{6,7},{7,6},{8,9},{9,8},{10,11... | collective-permute-start | bytes 786440 | tf_op jit(solution)/shard_map/ppermute | solution.py:570
  40.2 9.5 %collective-permute-start.6 = (bf16[128,1024]{1,0:T(8,128)(2,1)S(1)}, bf16[128,1024]{1,0:T(8,128)(2,1)S(1)}, u32[]{:S(2)}, u32[]{:S(2)}) collective-permute-start(bf16[128,1024]{1,0:T(8,128)(2,1)S(1)} %collective-permute-done.5), channel_id=1, source_target_pairs={{0,2},{2,0},{4,6},{6,4},{8,10},{10,8},{12,14},{14,12},{16,18},{18,... | collective-permute-start | bytes 786440 | tf_op jit(solution)/shard_map/ppermute | solution.py:573
  43.7 8.8 %collective-permute-start.9 = (bf16[128,1024]{1,0:T(8,128)(2,1)S(1)}, bf16[128,1024]{1,0:T(8,128)(2,1)S(1)}, u32[]{:S(2)}, u32[]{:S(2)}) collective-permute-start(bf16[128,1024]{1,0:T(8,128)(2,1)S(1)} %collective-permute-done.5), channel_id=1, source_target_pairs={{0,8},{2,10},{8,16},{10,18},{16,24},{18,26},{24,28},{26,30},{28,20... | collective-permute-start | bytes 786440 | tf_op jit(solution)/shard_map/ppermute | solution.py:578
  45.3 8.6 %collective-permute-start.8 = (bf16[128,1024]{1,0:T(8,128)(2,1)S(1)}, bf16[128,1024]{1,0:T(8,128)(2,1)S(1)}, u32[]{:S(2)}, u32[]{:S(2)}) collective-permute-start(bf16[128,1024]{1,0:T(8,128)(2,1)S(1)} %collective-permute-done.7), channel_id=1, source_target_pairs={{0,2},{2,0},{4,6},{6,4},{8,10},{10,8},{12,14},{14,12},{16,18},{18,... | collective-permute-start | bytes 786440 | tf_op jit(solution)/shard_map/ppermute | solution.py:573
  47.0 9.9 %collective-permute-start.11 = (bf16[128,1024]{1,0:T(8,128)(2,1)S(1)}, bf16[128,1024]{1,0:T(8,128)(2,1)S(1)}, u32[]{:S(2)}, u32[]{:S(2)}) collective-permute-start(bf16[128,1024]{1,0:T(8,128)(2,1)S(1)} %collective-permute-done.7), channel_id=1, source_target_pairs={{0,4},{2,6},{8,0},{10,2},{16,8},{18,10},{24,16},{26,18},{28,24},{3... | collective-permute-start | bytes 786440 | tf_op jit(solution)/shard_map/ppermute | solution.py:578
  49.0 15.9 %collective-permute-start.20 = (bf16[128,2048]{1,0:T(8,128)(2,1)S(1)}, bf16[128,2048]{1,0:T(8,128)(2,1)S(1)}, u32[]{:S(2)}, u32[]{:S(2)}) collective-permute-start(bf16[128,2048]{1,0:T(8,128)(2,1)S(1)} %slice.308), channel_id=1, source_target_pairs={{0,1},{1,0},{2,3},{3,2},{4,5},{5,4},{6,7},{7,6},{8,9},{9,8},{10,11... | collective-permute-start | bytes 1572872 | tf_op jit(solution)/shard_map/ppermute | solution.py:570
  49.7 13.0 %collective-permute-start.19 = (bf16[64,2048]{1,0:T(8,128)(2,1)S(1)}, bf16[64,2048]{1,0:T(8,128)(2,1)S(1)}, u32[]{:S(2)}, u32[]{:S(2)}) collective-permute-start(bf16[64,2048]{1,0:T(8,128)(2,1)S(1)} %collective-permute-done.18), channel_id=1, source_target_pairs={{0,2},{2,0},{4,6},{6,4},{8,10},{10,8},{12,14},{14,12},{16,18},{18,... | collective-permute-start | bytes 786440 | tf_op jit(solution)/shard_map/ppermute | solution.py:573
  53.9 8.7 %collective-permute-start.13 = (bf16[128,1024]{1,0:T(8,128)(2,1)S(1)}, bf16[128,1024]{1,0:T(8,128)(2,1)S(1)}, u32[]{:S(2)}, u32[]{:S(2)}) collective-permute-start(bf16[128,1024]{1,0:T(8,128)(2,1)S(1)} %collective-permute-done.9), channel_id=1, source_target_pairs={{0,8},{2,10},{8,16},{10,18},{16,24},{18,26},{24,28},{26,30},{28,20... | collective-permute-start | bytes 786440 | tf_op jit(solution)/shard_map/ppermute | solution.py:578
  56.9 5.9 %collective-permute-start.12 = (bf16[128,1024]{1,0:T(8,128)(2,1)S(1)}, bf16[128,1024]{1,0:T(8,128)(2,1)S(1)}, u32[]{:S(2)}, u32[]{:S(2)}) collective-permute-start(bf16[128,1024]{1,0:T(8,128)(2,1)S(1)} %collective-permute-done.11), channel_id=1, source_target_pairs={{0,2},{2,0},{4,6},{6,4},{8,10},{10,8},{12,14},{14,12},{16,18},{18,... | collective-permute-start | bytes 786440 | tf_op jit(solution)/shard_map/ppermute | solution.py:573
  64.9 31.0 %collective-permute-start.21 = (bf16[256,1024]{1,0:T(8,128)(2,1)S(1)}, bf16[256,1024]{1,0:T(8,128)(2,1)S(1)}, u32[]{:S(2)}, u32[]{:S(2)}) collective-permute-start(bf16[256,1024]{1,0:T(8,128)(2,1)S(1)} %constant_dynamic-slice_fusion.12), channel_id=1, source_target_pairs={{0,1},{1,0},{2,3},{3,2},{4,5},{5,4},{6,7},{7,6},{8,9},{9,8},{10,11... | collective-permute-start | bytes 1572872 | tf_op jit(solution)/shard_map/ppermute | solution.py:570
  89.6 16.3 %all-to-all-start = ((bf16[16,64,128]{2,1,0:T(8,128)(2,1)}), bf16[16,64,128]{2,1,0:T(8,128)(2,1)S(1)}, u32[]{:S(2)}, u32[]{:S(2)}) async-start(bf16[16,64,128]{2,1,0:T(8,128)(2,1)} %get-tuple-element.42), calls=%async_computation | async-start | bytes 524288 | tf_op jit(solution)/shard_map/all_to_all | solution.py:782
  95.9 86.2 %all-gather.8.cloned.1.call-start = ((), (), s32[]{:S(2)}) async-start(), calls=%async_computation.4 | async-start | bytes 4456448 | tf_op jit(solution)/shard_map/all_gather | solution.py:654
  96.0 10.6 %collective-permute-start.22 = (bf16[256,1024]{1,0:T(8,128)(2,1)S(1)}, bf16[256,1024]{1,0:T(8,128)(2,1)S(1)}, u32[]{:S(2)}, u32[]{:S(2)}) collective-permute-start(bf16[256,1024]{1,0:T(8,128)(2,1)S(1)} %collective-permute-done.21), channel_id=1, source_target_pairs={{0,2},{2,0},{4,6},{6,4},{8,10},{10,8},{12,14},{14,12},{16,18},{18,... | collective-permute-start | bytes 1572872 | tf_op jit(solution)/shard_map/ppermute | solution.py:573
  108.0 105.5 %all-gather.6.cloned.1.call-start = ((), (), s32[]{:S(2)}) async-start(), calls=%async_computation.3 | async-start | bytes 4456448 | tf_op jit(solution)/shard_map/all_gather | solution.py:654
  109.0 315.4 %all-gather.10.cloned.1.call-start = ((), (), s32[]{:S(2)}) async-start(), calls=%async_computation.5 | async-start | bytes 8912896 | tf_op jit(solution)/shard_map/all_gather | solution.py:654
  125.9 14.0 %collective-permute-start.23 = (bf16[256,1024]{1,0:T(8,128)(2,1)}, bf16[256,1024]{1,0:T(8,128)(2,1)S(1)}, u32[]{:S(2)}, u32[]{:S(2)}) collective-permute-start(bf16[256,1024]{1,0:T(8,128)(2,1)} %get-tuple-element.45), channel_id=1, source_target_pairs={{0,1},{1,0},{2,3},{3,2},{4,5},{5,4},{6,7},{7,6},{8,9},{9,8},{10,11... | collective-permute-start | bytes 1572872 | tf_op jit(solution)/shard_map/ppermute | solution.py:570
  139.9 12.9 %collective-permute-start.24 = (bf16[256,1024]{1,0:T(8,128)(2,1)S(1)}, bf16[256,1024]{1,0:T(8,128)(2,1)S(1)}, u32[]{:S(2)}, u32[]{:S(2)}) collective-permute-start(bf16[256,1024]{1,0:T(8,128)(2,1)S(1)} %get-tuple-element.46), channel_id=1, source_target_pairs={{0,1},{1,0},{2,3},{3,2},{4,5},{5,4},{6,7},{7,6},{8,9},{9,8},{10,11... | collective-permute-start | bytes 1572872 | tf_op jit(solution)/shard_map/ppermute | solution.py:570
  141.4 17.0 %collective-permute-start.27 = (bf16[256,1024]{1,0:T(8,128)(2,1)S(1)}, bf16[256,1024]{1,0:T(8,128)(2,1)S(1)}, u32[]{:S(2)}, u32[]{:S(2)}) collective-permute-start(bf16[256,1024]{1,0:T(8,128)(2,1)S(1)} %collective-permute-done.23), channel_id=1, source_target_pairs={{0,4},{2,6},{4,0},{6,2},{8,12},{10,14},{12,8},{14,10},{16,20},{18,... | collective-permute-start | bytes 1572872 | tf_op jit(solution)/shard_map/ppermute | solution.py:573
  143.6 25.4 %collective-permute-start.25 = (bf16[256,1024]{1,0:T(8,128)(2,1)S(1)}, bf16[256,1024]{1,0:T(8,128)(2,1)S(1)}, u32[]{:S(2)}, u32[]{:S(2)}) collective-permute-start(bf16[256,1024]{1,0:T(8,128)(2,1)S(1)} %collective-permute-done.23), channel_id=1, source_target_pairs={{0,2},{2,0},{4,6},{6,4},{8,10},{10,8},{12,14},{14,12},{16,18},{18,... | collective-permute-start | bytes 1572872 | tf_op jit(solution)/shard_map/ppermute | solution.py:573
  152.9 6.4 %collective-permute-start.31 = (bf16[128,1024]{1,0:T(8,128)(2,1)S(1)}, bf16[128,1024]{1,0:T(8,128)(2,1)S(1)}, u32[]{:S(2)}, u32[]{:S(2)}) collective-permute-start(bf16[128,1024]{1,0:T(8,128)(2,1)S(1)} %constant_dynamic-slice_fusion.8), channel_id=1, source_target_pairs={{0,1},{1,0},{2,3},{3,2},{4,5},{5,4},{6,7},{7,6},{8,9},{9,8},{10,11... | collective-permute-start | bytes 786440 | tf_op jit(solution)/shard_map/ppermute | solution.py:570
  154.3 14.6 %collective-permute-start.28 = (bf16[256,1024]{1,0:T(8,128)(2,1)S(1)}, bf16[256,1024]{1,0:T(8,128)(2,1)S(1)}, u32[]{:S(2)}, u32[]{:S(2)}) collective-permute-start(bf16[256,1024]{1,0:T(8,128)(2,1)S(1)} %collective-permute-done.24), channel_id=1, source_target_pairs={{0,4},{2,6},{4,0},{6,2},{8,12},{10,14},{12,8},{14,10},{16,20},{18,... | collective-permute-start | bytes 1572872 | tf_op jit(solution)/shard_map/ppermute | solution.py:573
  156.1 14.7 %collective-permute-start.26 = (bf16[256,1024]{1,0:T(8,128)(2,1)S(1)}, bf16[256,1024]{1,0:T(8,128)(2,1)S(1)}, u32[]{:S(2)}, u32[]{:S(2)}) collective-permute-start(bf16[256,1024]{1,0:T(8,128)(2,1)S(1)} %collective-permute-done.24), channel_id=1, source_target_pairs={{0,2},{2,0},{4,6},{6,4},{8,10},{10,8},{12,14},{14,12},{16,18},{18,... | collective-permute-start | bytes 1572872 | tf_op jit(solution)/shard_map/ppermute | solution.py:573
  158.4 10.5 %collective-permute-start.29 = (bf16[256,1024]{1,0:T(8,128)(2,1)S(1)}, bf16[256,1024]{1,0:T(8,128)(2,1)S(1)}, u32[]{:S(2)}, u32[]{:S(2)}) collective-permute-start(bf16[256,1024]{1,0:T(8,128)(2,1)S(1)} %collective-permute-done.27), channel_id=1, source_target_pairs={{0,2},{2,0},{4,6},{6,4},{8,10},{10,8},{12,14},{14,12},{16,18},{18,... | collective-permute-start | bytes 1572872 | tf_op jit(solution)/shard_map/ppermute | solution.py:573
  159.3 149.4 %collective-permute-start.32 = (bf16[256,3072]{1,0:T(8,128)(2,1)}, bf16[256,3072]{1,0:T(8,128)(2,1)}, u32[]{:S(2)}, u32[]{:S(2)}) collective-permute-start(bf16[256,3072]{1,0:T(8,128)(2,1)} %constant_dynamic-slice_fusion.9), channel_id=1, source_target_pairs={{0,1},{1,0},{2,3},{3,2},{4,5},{5,4},{6,7},{7,6},{8,9},{9,8},{10,11... | collective-permute-start | bytes 4718600 | tf_op jit(solution)/shard_map/ppermute | solution.py:570
  224.2 8.7 %collective-permute-start.57 = (bf16[512,256]{1,0:T(8,128)(2,1)S(1)}, bf16[512,256]{1,0:T(8,128)(2,1)S(1)}, u32[]{:S(2)}, u32[]{:S(2)}) collective-permute-start(bf16[512,256]{1,0:T(8,128)(2,1)S(1)} %dynamic-slice_convert_fusion.3), channel_id=1, source_target_pairs={{0,1},{1,0},{2,3},{3,2},{4,5},{5,4},{6,7},{7,6},{8,9},{9,8},{10,11... | collective-permute-start | bytes 786440 | tf_op jit(solution)/shard_map/ppermute | solution.py:570
  229.9 8.4 %collective-permute-start.58 = (bf16[128,1024]{1,0:T(8,128)(2,1)S(1)}, bf16[128,1024]{1,0:T(8,128)(2,1)S(1)}, u32[]{:S(2)}, u32[]{:S(2)}) collective-permute-start(bf16[128,1024]{1,0:T(8,128)(2,1)S(1)} %dynamic-slice_convert_fusion.2), channel_id=1, source_target_pairs={{0,1},{1,0},{2,3},{3,2},{4,5},{5,4},{6,7},{7,6},{8,9},{9,8},{10,11... | collective-permute-start | bytes 786440 | tf_op jit(solution)/shard_map/ppermute | solution.py:570
  248.6 16.0 %collective-permute-start.37 = (bf16[2,8,32,1024]{3,2,1,0:T(8,128)(2,1)S(1)}, bf16[2,8,32,1024]{3,2,1,0:T(8,128)(2,1)}, u32[]{:S(2)}, u32[]{:S(2)}) collective-permute-start(bf16[2,8,32,1024]{3,2,1,0:T(8,128)(2,1)S(1)} %fusion.23), channel_id=1, source_target_pairs={{0,2},{2,0},{4,6},{6,4},{8,10},{10,8},{12,14},{14,12},{16,18},{18,... | collective-permute-start | bytes 3145736 | tf_op jit(solution)/shard_map/ppermute | solution.py:573
  252.0 25.0 %all-to-all-start.1 = ((bf16[16,64,128]{2,1,0:T(8,128)(2,1)}), bf16[16,64,128]{2,1,0:T(8,128)(2,1)S(1)}, u32[]{:S(2)}, u32[]{:S(2)}) async-start(bf16[16,64,128]{2,1,0:T(8,128)(2,1)} %bitcast.21), calls=%async_computation.1 | async-start | bytes 524288 | tf_op jit(solution)/shard_map/all_to_all | solution.py:811
  268.3 32.2 %collective-permute-start.38 = (bf16[8,32,1024]{2,1,0:T(8,128)(2,1)S(1)}, bf16[8,32,1024]{2,1,0:T(8,128)(2,1)}, u32[]{:S(2)}, u32[]{:S(2)}) collective-permute-start(bf16[8,32,1024]{2,1,0:T(8,128)(2,1)S(1)} %fusion.42), channel_id=1, source_target_pairs={{0,1},{1,0},{2,3},{3,2},{4,5},{5,4},{6,7},{7,6},{8,9},{9,8},{10,11... | collective-permute-start | bytes 1572872 | tf_op jit(solution)/shard_map/ppermute | solution.py:570
  296.8 36.9 %all-to-all-start.2 = ((bf16[16,192,128]{2,1,0:T(8,128)(2,1)}), bf16[16,192,128]{2,1,0:T(8,128)(2,1)S(1)}, u32[]{:S(2)}, u32[]{:S(2)}) async-start(bf16[16,192,128]{2,1,0:T(8,128)(2,1)} %get-tuple-element.54), calls=%async_computation.2 | async-start | bytes 1572864 | tf_op jit(solution)/shard_map/all_to_all | solution.py:823
  302.2 13.1 %collective-permute-start.39 = (bf16[1,4,32,1024]{3,2,1,0:T(8,128)(2,1)S(1)}, bf16[1,4,32,1024]{3,2,1,0:T(8,128)(2,1)S(1)}, u32[]{:S(2)}, u32[]{:S(2)}) collective-permute-start(bf16[1,4,32,1024]{3,2,1,0:T(8,128)(2,1)S(1)} %fusion.59), channel_id=1, source_target_pairs={{0,4},{2,6},{4,0},{6,2},{8,12},{10,14},{12,8},{14,10},{16,20},{18,... | collective-permute-start | bytes 786440 | tf_op jit(solution)/shard_map/ppermute | solution.py:573
  307.3 8.7 %collective-permute-start.36 = (bf16[192,512]{1,0:T(8,128)(2,1)S(1)}, bf16[192,512]{1,0:T(8,128)(2,1)S(1)}, u32[]{:S(2)}, u32[]{:S(2)}) collective-permute-start(bf16[192,512]{1,0:T(8,128)(2,1)S(1)} %dynamic-slice_convert_fusion.4), channel_id=1, source_target_pairs={{0,1},{1,0},{2,3},{3,2},{4,5},{5,4},{6,7},{7,6},{8,9},{9,8},{10,11... | collective-permute-start | bytes 589832 | tf_op jit(solution)/shard_map/ppermute | solution.py:570
  308.7 31.0 %collective-permute-start.35 = (bf16[256,3072]{1,0:T(8,128)(2,1)}, bf16[256,3072]{1,0:T(8,128)(2,1)}, u32[]{:S(2)}, u32[]{:S(2)}) collective-permute-start(bf16[256,3072]{1,0:T(8,128)(2,1)} %collective-permute-done.32), channel_id=1, source_target_pairs={{0,2},{2,0},{4,6},{6,4},{8,10},{10,8},{12,14},{14,12},{16,18},{18,... | collective-permute-start | bytes 4718600 | tf_op jit(solution)/shard_map/ppermute | solution.py:573
  315.4 15.0 %collective-permute-start.40 = (bf16[1,2,32,1024]{3,2,1,0:T(8,128)(2,1)S(1)}, bf16[1,2,32,1024]{3,2,1,0:T(8,128)(2,1)S(1)}, u32[]{:S(2)}, u32[]{:S(2)}) collective-permute-start(bf16[1,2,32,1024]{3,2,1,0:T(8,128)(2,1)S(1)} %fusion.75), channel_id=1, source_target_pairs={{0,8},{2,10},{4,12},{6,14},{8,0},{10,2},{12,4},{14,6},{16,24},{18,... | collective-permute-start | bytes 393224 | tf_op jit(solution)/shard_map/ppermute | solution.py:573
  330.5 8.6 %collective-permute-start.41 = (bf16[1,1,32,1024]{3,2,1,0:T(8,128)(2,1)S(1)}, bf16[1,1,32,1024]{3,2,1,0:T(8,128)(2,1)S(1)}, u32[]{:S(2)}, u32[]{:S(2)}) collective-permute-start(bf16[1,1,32,1024]{3,2,1,0:T(8,128)(2,1)S(1)} %dynamic-slice_convert_fusion.5), channel_id=1, source_target_pairs={{0,16},{2,18},{4,20},{6,22},{8,24},{10,26},{12,28},{14,30},{16,0},... | collective-permute-start | bytes 196616 | tf_op jit(solution)/shard_map/ppermute | solution.py:573
  339.2 12.5 %collective-permute-start.42 = (bf16[256,512]{1,0:T(8,128)(2,1)S(1)}, bf16[256,512]{1,0:T(8,128)(2,1)S(1)}, u32[]{:S(2)}, u32[]{:S(2)}) collective-permute-start(bf16[256,512]{1,0:T(8,128)(2,1)S(1)} %pad_maximum_fusion.2), channel_id=1, source_target_pairs={{0,2},{2,0},{4,6},{6,4},{8,10},{10,8},{12,14},{14,12},{16,18},{18,... | collective-permute-start | bytes 786440 | tf_op jit(solution)/shard_map/ppermute | solution.py:573
  339.2 9.4 %collective-permute-start.43 = (bf16[256,512]{1,0:T(8,128)(2,1)S(1)}, bf16[256,512]{1,0:T(8,128)(2,1)S(1)}, u32[]{:S(2)}, u32[]{:S(2)}) collective-permute-start(bf16[256,512]{1,0:T(8,128)(2,1)S(1)} %pad_maximum_fusion.2), channel_id=1, source_target_pairs={{0,8},{2,10},{8,16},{10,18},{16,24},{18,26},{24,28},{26,30},{28,20... | collective-permute-start | bytes 786440 | tf_op jit(solution)/shard_map/ppermute | solution.py:578
  344.8 56.6 %collective-permute-start.33 = (bf16[1024,1024]{1,0:T(8,128)(2,1)S(1)}, bf16[1024,1024]{1,0:T(8,128)(2,1)}, u32[]{:S(2)}, u32[]{:S(2)}) collective-permute-start(bf16[1024,1024]{1,0:T(8,128)(2,1)S(1)} %copy-done.12), channel_id=1, source_target_pairs={{0,1},{1,0},{2,3},{3,2},{4,5},{5,4},{6,7},{7,6},{8,9},{9,8},{10,11... | collective-permute-start | bytes 6291464 | tf_op jit(solution)/shard_map/ppermute | solution.py:570
  348.0 11.1 %collective-permute-start.45 = (bf16[256,512]{1,0:T(8,128)(2,1)S(1)}, bf16[256,512]{1,0:T(8,128)(2,1)S(1)}, u32[]{:S(2)}, u32[]{:S(2)}) collective-permute-start(bf16[256,512]{1,0:T(8,128)(2,1)S(1)} %pad_maximum_fusion.2), channel_id=1, source_target_pairs={{0,4},{2,6},{8,0},{10,2},{16,8},{18,10},{24,16},{26,18},{28,24},{3... | collective-permute-start | bytes 786440 | tf_op jit(solution)/shard_map/ppermute | solution.py:578
  348.6 17.1 %collective-permute-start.44 = (bf16[256,512]{1,0:T(8,128)(2,1)S(1)}, bf16[256,512]{1,0:T(8,128)(2,1)S(1)}, u32[]{:S(2)}, u32[]{:S(2)}) collective-permute-start(bf16[256,512]{1,0:T(8,128)(2,1)S(1)} %collective-permute-done.43), channel_id=1, source_target_pairs={{0,2},{2,0},{4,6},{6,4},{8,10},{10,8},{12,14},{14,12},{16,18},{18,... | collective-permute-start | bytes 786440 | tf_op jit(solution)/shard_map/ppermute | solution.py:573
  350.6 15.8 %collective-permute-start.47 = (bf16[256,512]{1,0:T(8,128)(2,1)S(1)}, bf16[256,512]{1,0:T(8,128)(2,1)S(1)}, u32[]{:S(2)}, u32[]{:S(2)}) collective-permute-start(bf16[256,512]{1,0:T(8,128)(2,1)S(1)} %collective-permute-done.43), channel_id=1, source_target_pairs={{0,8},{2,10},{8,16},{10,18},{16,24},{18,26},{24,28},{26,30},{28,20... | collective-permute-start | bytes 786440 | tf_op jit(solution)/shard_map/ppermute | solution.py:578
  351.6 5.9 %collective-permute-start.61 = (f32[1,11264]{1,0:T(1,128)S(1)}, f32[1,11264]{1,0:T(1,128)S(1)}, u32[]{:S(2)}, u32[]{:S(2)}) collective-permute-start(f32[1,11264]{1,0:T(1,128)S(1)} %add.622), channel_id=1, source_target_pairs={{0,8},{2,10},{4,12},{6,14},{8,0},{10,2},{12,4},{14,6},{16,24},{18,... | collective-permute-start | bytes 135176 | tf_op jit(solution)/shard_map/ppermute | solution.py:573
  357.6 5.0 %collective-permute-start.62 = (f32[1,11264]{1,0:T(1,128)S(1)}, f32[1,11264]{1,0:T(1,128)S(1)}, u32[]{:S(2)}, u32[]{:S(2)}) collective-permute-start(f32[1,11264]{1,0:T(1,128)S(1)} %add.623), channel_id=1, source_target_pairs={{0,16},{2,18},{4,20},{6,22},{8,24},{10,26},{12,28},{14,30},{16,0},... | collective-permute-start | bytes 135176 | tf_op jit(solution)/shard_map/ppermute | solution.py:573
  359.1 7.3 %collective-permute-start.46 = (bf16[256,512]{1,0:T(8,128)(2,1)S(1)}, bf16[256,512]{1,0:T(8,128)(2,1)S(1)}, u32[]{:S(2)}, u32[]{:S(2)}) collective-permute-start(bf16[256,512]{1,0:T(8,128)(2,1)S(1)} %collective-permute-done.45), channel_id=1, source_target_pairs={{0,2},{2,0},{4,6},{6,4},{8,10},{10,8},{12,14},{14,12},{16,18},{18,... | collective-permute-start | bytes 786440 | tf_op jit(solution)/shard_map/ppermute | solution.py:573
  362.6 7.4 %collective-permute-start.49 = (bf16[256,512]{1,0:T(8,128)(2,1)S(1)}, bf16[256,512]{1,0:T(8,128)(2,1)S(1)}, u32[]{:S(2)}, u32[]{:S(2)}) collective-permute-start(bf16[256,512]{1,0:T(8,128)(2,1)S(1)} %collective-permute-done.45), channel_id=1, source_target_pairs={{0,4},{2,6},{8,0},{10,2},{16,8},{18,10},{24,16},{26,18},{28,24},{3... | collective-permute-start | bytes 786440 | tf_op jit(solution)/shard_map/ppermute | solution.py:578
  365.7 27.8 %collective-permute-start.63 = (f32[1,11264]{1,0:T(1,128)S(1)}, f32[1,11264]{1,0:T(1,128)S(1)}, u32[]{:S(2)}, u32[]{:S(2)}) collective-permute-start(f32[1,11264]{1,0:T(1,128)S(1)} %add.624), channel_id=1, source_target_pairs={{0,1},{1,0},{2,3},{3,2},{4,5},{5,4},{6,7},{7,6},{8,9},{9,8},{10,11... | collective-permute-start | bytes 135176 | tf_op jit(solution)/shard_map/ppermute | solution.py:570
  366.3 34.3 %collective-permute-start.48 = (bf16[256,512]{1,0:T(8,128)(2,1)S(1)}, bf16[256,512]{1,0:T(8,128)(2,1)S(1)}, u32[]{:S(2)}, u32[]{:S(2)}) collective-permute-start(bf16[256,512]{1,0:T(8,128)(2,1)S(1)} %collective-permute-done.47), channel_id=1, source_target_pairs={{0,2},{2,0},{4,6},{6,4},{8,10},{10,8},{12,14},{14,12},{16,18},{18,... | collective-permute-start | bytes 786440 | tf_op jit(solution)/shard_map/ppermute | solution.py:573
  366.4 34.2 %collective-permute-start.51 = (bf16[256,512]{1,0:T(8,128)(2,1)S(1)}, bf16[256,512]{1,0:T(8,128)(2,1)S(1)}, u32[]{:S(2)}, u32[]{:S(2)}) collective-permute-start(bf16[256,512]{1,0:T(8,128)(2,1)S(1)} %collective-permute-done.47), channel_id=1, source_target_pairs={{0,8},{2,10},{8,16},{10,18},{16,24},{18,26},{24,28},{26,30},{28,20... | collective-permute-start | bytes 786440 | tf_op jit(solution)/shard_map/ppermute | solution.py:578
  370.0 31.9 %collective-permute-start.50 = (bf16[256,512]{1,0:T(8,128)(2,1)S(1)}, bf16[256,512]{1,0:T(8,128)(2,1)S(1)}, u32[]{:S(2)}, u32[]{:S(2)}) collective-permute-start(bf16[256,512]{1,0:T(8,128)(2,1)S(1)} %collective-permute-done.49), channel_id=1, source_target_pairs={{0,2},{2,0},{4,6},{6,4},{8,10},{10,8},{12,14},{14,12},{16,18},{18,... | collective-permute-start | bytes 786440 | tf_op jit(solution)/shard_map/ppermute | solution.py:573
  393.6 7.7 %collective-permute-start.53 = (bf16[256,512]{1,0:T(8,128)(2,1)S(1)}, bf16[256,512]{1,0:T(8,128)(2,1)S(1)}, u32[]{:S(2)}, u32[]{:S(2)}) collective-permute-start(bf16[256,512]{1,0:T(8,128)(2,1)S(1)} %collective-permute-done.49), channel_id=1, source_target_pairs={{0,4},{2,6},{8,0},{10,2},{16,8},{18,10},{24,16},{26,18},{28,24},{3... | collective-permute-start | bytes 786440 | tf_op jit(solution)/shard_map/ppermute | solution.py:578
  400.6 8.7 %collective-permute-start.52 = (bf16[256,512]{1,0:T(8,128)(2,1)S(1)}, bf16[256,512]{1,0:T(8,128)(2,1)S(1)}, u32[]{:S(2)}, u32[]{:S(2)}) collective-permute-start(bf16[256,512]{1,0:T(8,128)(2,1)S(1)} %collective-permute-done.51), channel_id=1, source_target_pairs={{0,2},{2,0},{4,6},{6,4},{8,10},{10,8},{12,14},{14,12},{16,18},{18,... | collective-permute-start | bytes 786440 | tf_op jit(solution)/shard_map/ppermute | solution.py:573
  400.6 8.7 %collective-permute-start.55 = (bf16[256,512]{1,0:T(8,128)(2,1)S(1)}, bf16[256,512]{1,0:T(8,128)(2,1)S(1)}, u32[]{:S(2)}, u32[]{:S(2)}) collective-permute-start(bf16[256,512]{1,0:T(8,128)(2,1)S(1)} %collective-permute-done.51), channel_id=1, source_target_pairs={{0,8},{2,10},{8,16},{10,18},{16,24},{18,26},{24,28},{26,30},{28,20... | collective-permute-start | bytes 786440 | tf_op jit(solution)/shard_map/ppermute | solution.py:578
  401.3 8.1 %collective-permute-start.54 = (bf16[256,512]{1,0:T(8,128)(2,1)S(1)}, bf16[256,512]{1,0:T(8,128)(2,1)S(1)}, u32[]{:S(2)}, u32[]{:S(2)}) collective-permute-start(bf16[256,512]{1,0:T(8,128)(2,1)S(1)} %collective-permute-done.53), channel_id=1, source_target_pairs={{0,2},{2,0},{4,6},{6,4},{8,10},{10,8},{12,14},{14,12},{16,18},{18,... | collective-permute-start | bytes 786440 | tf_op jit(solution)/shard_map/ppermute | solution.py:573
  401.3 20.9 %collective-permute-start.34 = (bf16[1024,1024]{1,0:T(8,128)(2,1)}, bf16[1024,1024]{1,0:T(8,128)(2,1)S(1)}, u32[]{:S(2)}, u32[]{:S(2)}) collective-permute-start(bf16[1024,1024]{1,0:T(8,128)(2,1)} %collective-permute-done.33), channel_id=1, source_target_pairs={{0,2},{2,0},{4,6},{6,4},{8,10},{10,8},{12,14},{14,12},{16,18},{18,... | collective-permute-start | bytes 6291464 | tf_op jit(solution)/shard_map/ppermute | solution.py:573
  (44 other events, 755.3 us)
Sparse Core Ops, SparseCore 0:
  108.2 53.4 all-gather.7
  163.8 49.7 all-gather.5
  243.6 89.8 all-gather.9
